TPU v7x, 32 devices: a whole 2x2x4 slice. The times are simulated.
32 devices in a mesh: ctx: 8 (over z, core), fsdp: 4 (over y, x).
Axes of the slice: x: 2, y: 2, z: 4, core: 2. Of those that a mesh axis runs over, the one named last changes fastest.
Arguments:
- tokens: bfloat16 [4, 4096, 768], P('fsdp', 'ctx'), may hold values from -6 to 6
- encoder_states: bfloat16 [4, 1500, 768], P('fsdp'), may hold values from -6 to 6
- lengths: int32 [4], P('fsdp'), may hold values from 1024 to 4096, as said below
- cotangent: bfloat16 [4, 4096, 768], P('fsdp', 'ctx'), may hold values from -6 to 6
- first_gain: bfloat16 [768], P('fsdp'), may hold values from 0.5 to 1.5
- first_shift: bfloat16 [768], P('fsdp'), may hold values from -1.5 to 1.5
- query_weight: bfloat16 [768, 768], P('fsdp'), may hold values from -0.21875 to 0.21875
- query_bias: bfloat16 [768], P('fsdp'), may hold values from -1.5 to 1.5
- key_weight: bfloat16 [768, 768], P('fsdp'), may hold values from -0.21875 to 0.21875
- value_weight: bfloat16 [768, 768], P('fsdp'), may hold values from -0.21875 to 0.21875
- value_bias: bfloat16 [768], P('fsdp'), may hold values from -1.5 to 1.5
- self_out_weight: bfloat16 [768, 768], P('fsdp'), may hold values from -3.5 to 3.5
- self_out_bias: bfloat16 [768], P('fsdp'), may hold values from -1.5 to 1.5
- second_gain: bfloat16 [768], P('fsdp'), may hold values from 0.5 to 1.5
- second_shift: bfloat16 [768], P('fsdp'), may hold values from -1.5 to 1.5
- cross_query_weight: bfloat16 [768, 768], P('fsdp'), may hold values from -0.21875 to 0.21875
- cross_query_bias: bfloat16 [768], P('fsdp'), may hold values from -1.5 to 1.5
- cross_key_weight: bfloat16 [768, 768], P('fsdp'), may hold values from -0.21875 to 0.21875
- cross_value_weight: bfloat16 [768, 768], P('fsdp'), may hold values from -0.21875 to 0.21875
- cross_value_bias: bfloat16 [768], P('fsdp'), may hold values from -1.5 to 1.5
- cross_out_weight: bfloat16 [768, 768], P('fsdp'), may hold values from -3.5 to 3.5
- cross_out_bias: bfloat16 [768], P('fsdp'), may hold values from -1.5 to 1.5
- third_gain: bfloat16 [768], P('fsdp'), may hold values from 0.5 to 1.5
- third_shift: bfloat16 [768], P('fsdp'), may hold values from -1.5 to 1.5
- expand_weight: bfloat16 [768, 3072], P('fsdp'), may hold values from -0.21875 to 0.21875
- expand_bias: bfloat16 [3072], P('fsdp'), may hold values from -1.5 to 1.5
- reduce_weight: bfloat16 [3072, 768], P('fsdp'), may hold values from -0.109375 to 0.109375
- reduce_bias: bfloat16 [768], P('fsdp'), may hold values from -2.5 to 2.5
Outputs:
- layer_out: float32 [4, 4096, 768], P('fsdp', 'ctx')
- token_grads: float32 [4, 4096, 768], P('fsdp', 'ctx')
- encoder_grads: float32 [4, 1500, 768], P('fsdp')
- gradient_first_gain: float32 [768], P('fsdp')
- gradient_first_shift: float32 [768], P('fsdp')
- gradient_query_weight: float32 [768, 768], P('fsdp')
- gradient_query_bias: float32 [768], P('fsdp')
- gradient_key_weight: float32 [768, 768], P('fsdp')
- gradient_value_weight: float32 [768, 768], P('fsdp')
- gradient_value_bias: float32 [768], P('fsdp')
- gradient_self_out_weight: float32 [768, 768], P('fsdp')
- gradient_self_out_bias: float32 [768], P('fsdp')
- gradient_second_gain: float32 [768], P('fsdp')
- gradient_second_shift: float32 [768], P('fsdp')
- gradient_cross_query_weight: float32 [768, 768], P('fsdp')
- gradient_cross_query_bias: float32 [768], P('fsdp')
- gradient_cross_key_weight: float32 [768, 768], P('fsdp')
- gradient_cross_value_weight: float32 [768, 768], P('fsdp')
- gradient_cross_value_bias: float32 [768], P('fsdp')
- gradient_cross_out_weight: float32 [768, 768], P('fsdp')
- gradient_cross_out_bias: float32 [768], P('fsdp')
- gradient_third_gain: float32 [768], P('fsdp')
- gradient_third_shift: float32 [768], P('fsdp')
- gradient_expand_weight: float32 [768, 3072], P('fsdp')
- gradient_expand_bias: float32 [3072], P('fsdp')
- gradient_reduce_weight: float32 [3072, 768], P('fsdp')
- gradient_reduce_bias: float32 [768], P('fsdp')
Inputs may be any that keep to these rules, and one draw needn't show every extreme that they name: `lengths`: real tokens of each slot fill its first positions; in every draw one slot is full and one holds exactly 1024 real tokens.
All inputs are finite; a program needn't handle non-finite values.
Results may differ from a plain program's by a relative error of at most 0.033.
Values may be sent and summed in bfloat16 or wider, within the bound.
A program may use at most 320 MiB of HBM per device.

v0:
```python
import math

import jax
import jax.numpy as jnp
from jax import lax
from jax.sharding import PartitionSpec as P

HEADS = 12
HEAD_DIM = 64


eps = 1e-05
masked = -1e30


def layer_norm(input_rows, norm_gain, norm_shift):
    centre = jnp.mean(input_rows, axis=-1, keepdims=True)
    centered = input_rows - centre
    spread = jnp.mean(centered * centered, axis=-1, keepdims=True)
    return centered * lax.rsqrt(spread + eps) * norm_gain + norm_shift


def gelu_exact(input_rows):
    return jax.nn.gelu(input_rows, approximate=False)


def split_heads(input_rows):
    return input_rows.reshape(input_rows.shape[:-1] + (HEADS, HEAD_DIM))


def merge_heads(input_rows):
    return input_rows.reshape(input_rows.shape[:-2] + (HEADS * HEAD_DIM,))


def forward_mult(input_rows, weight_matrix):
    return jnp.einsum("vrw,wk->vrk", input_rows, weight_matrix, preferred_element_type=jnp.float32)


def backward_product(incoming_gradient, weight_matrix):
    return jnp.einsum(
        "zax,qx->zaq", incoming_gradient, weight_matrix, preferred_element_type=jnp.float32
    )


def weight_grad(input_rows, incoming_gradient):
    return jnp.einsum(
        "qxy,qxg->yg", input_rows, incoming_gradient, preferred_element_type=jnp.float32
    )


def bias_grad(incoming_gradient):
    return jnp.sum(incoming_gradient.astype(jnp.float32), axis=(0, 1))


def allowed_mask(query_pos, key_pos, lengths):
    causal = key_pos[None, None, None, :] <= query_pos[None, None, :, None]
    inside = key_pos[None, None, None, :] < lengths[:, None, None, None]
    return causal & inside


def regroup_rows(blocks):
    return jnp.swapaxes(blocks, 0, 1).reshape(
        blocks.shape[1], blocks.shape[0] * blocks.shape[2], blocks.shape[3]
    )


def fold_update(fold_carry, key_block, value_block, query_rows, query_pos, key_pos, lengths):
    running, row_top, row_total = fold_carry
    score_scale = HEAD_DIM ** (-0.5)
    scores = (
        jnp.einsum(
            "sqhe,skhe->shqk",
            split_heads(query_rows),
            split_heads(key_block),
            preferred_element_type=jnp.float32,
        )
        * score_scale
    )
    allowed = allowed_mask(query_pos, key_pos, lengths)
    new_top = jnp.maximum(row_top, jnp.max(jnp.where(allowed, scores, masked), axis=-1))
    weights = jnp.where(allowed, jnp.exp(scores - new_top[..., None]), 0.0)
    factor = jnp.exp(row_top - new_top)
    row_total = row_total * factor + jnp.sum(weights, axis=-1)
    mixed_block = jnp.einsum(
        "shqk,skhe->sqhe",
        weights.astype(jnp.bfloat16),
        split_heads(value_block),
        preferred_element_type=jnp.float32,
    )
    running = running * jnp.swapaxes(factor, 1, 2)[..., None] + mixed_block
    return (running, new_top, row_total)


def tile_grads(query_rows, dout_rows, row_lse, row_delta, key_rows, value_rows, allowed):
    score_scale = HEAD_DIM ** (-0.5)
    query_heads = split_heads(query_rows)
    dout_heads = split_heads(dout_rows)
    key_heads = split_heads(key_rows)
    value_heads = split_heads(value_rows)
    scores = (
        jnp.einsum("sqhe,skhe->shqk", query_heads, key_heads, preferred_element_type=jnp.float32)
        * score_scale
    )
    probability = jnp.where(allowed, jnp.exp(scores - row_lse[..., None]), 0.0)
    value_part = jnp.einsum(
        "shqk,sqhe->skhe",
        probability.astype(jnp.bfloat16),
        dout_heads,
        preferred_element_type=jnp.float32,
    )
    prob_grad = jnp.einsum(
        "sqhe,skhe->shqk", dout_heads, value_heads, preferred_element_type=jnp.float32
    )
    score_grad = (probability * (prob_grad - row_delta[..., None])).astype(jnp.bfloat16)
    query_part = (
        jnp.einsum("shqk,skhe->sqhe", score_grad, key_heads, preferred_element_type=jnp.float32)
        * score_scale
    )
    key_part = (
        jnp.einsum("shqk,sqhe->skhe", score_grad, query_heads, preferred_element_type=jnp.float32)
        * score_scale
    )
    return (merge_heads(query_part), merge_heads(key_part), merge_heads(value_part))


def cross_attention_forward(slot_items):
    query_rows, key_rows, value_rows = slot_items
    score_scale = HEAD_DIM ** (-0.5)
    scores = (
        jnp.einsum(
            "qhe,khe->hqk",
            split_heads(query_rows),
            split_heads(key_rows),
            preferred_element_type=jnp.float32,
        )
        * score_scale
    )
    row_top = jnp.max(scores, axis=-1, keepdims=True)
    weights = jnp.exp(scores - row_top)
    probability = weights / jnp.sum(weights, axis=-1, keepdims=True)
    return merge_heads(
        jnp.einsum(
            "hqk,khe->qhe",
            probability.astype(jnp.bfloat16),
            split_heads(value_rows),
            preferred_element_type=jnp.float32,
        )
    )


def cross_backward(slot_items):
    query_rows, key_rows, value_rows, dout_rows = slot_items
    score_scale = HEAD_DIM ** (-0.5)
    query_heads = split_heads(query_rows)
    key_heads = split_heads(key_rows)
    value_heads = split_heads(value_rows)
    dout_heads = split_heads(dout_rows)
    scores = (
        jnp.einsum("qhe,khe->hqk", query_heads, key_heads, preferred_element_type=jnp.float32)
        * score_scale
    )
    row_top = jnp.max(scores, axis=-1, keepdims=True)
    weights = jnp.exp(scores - row_top)
    probability = weights / jnp.sum(weights, axis=-1, keepdims=True)
    value_part = jnp.einsum(
        "hqk,qhe->khe",
        probability.astype(jnp.bfloat16),
        dout_heads,
        preferred_element_type=jnp.float32,
    )
    prob_grad = jnp.einsum(
        "qhe,khe->hqk", dout_heads, value_heads, preferred_element_type=jnp.float32
    )
    row_delta = jnp.sum(probability * prob_grad, axis=-1, keepdims=True)
    score_grad = (probability * (prob_grad - row_delta)).astype(jnp.bfloat16)
    query_part = (
        jnp.einsum("hqk,khe->qhe", score_grad, key_heads, preferred_element_type=jnp.float32)
        * score_scale
    )
    key_part = (
        jnp.einsum("hqk,qhe->khe", score_grad, query_heads, preferred_element_type=jnp.float32)
        * score_scale
    )
    return (merge_heads(query_part), merge_heads(key_part), merge_heads(value_part))


def body(
    tokens,
    encoder_states,
    lengths,
    cotangent,
    first_gain,
    first_shift,
    query_weight,
    query_bias,
    key_weight,
    value_weight,
    value_bias,
    self_out_weight,
    self_out_bias,
    second_gain,
    second_shift,
    cross_query_weight,
    cross_query_bias,
    cross_key_weight,
    cross_value_weight,
    cross_value_bias,
    cross_out_weight,
    cross_out_bias,
    third_gain,
    third_shift,
    expand_weight,
    expand_bias,
    reduce_weight,
    reduce_bias,
):
    gathered = (
        lax.all_gather(first_gain, "fsdp", axis=0, tiled=True),
        lax.all_gather(first_shift, "fsdp", axis=0, tiled=True),
        lax.all_gather(query_weight, "fsdp", axis=0, tiled=True),
        lax.all_gather(query_bias, "fsdp", axis=0, tiled=True),
        lax.all_gather(key_weight, "fsdp", axis=0, tiled=True),
        lax.all_gather(value_weight, "fsdp", axis=0, tiled=True),
        lax.all_gather(value_bias, "fsdp", axis=0, tiled=True),
        lax.all_gather(self_out_weight, "fsdp", axis=0, tiled=True),
        lax.all_gather(self_out_bias, "fsdp", axis=0, tiled=True),
        lax.all_gather(second_gain, "fsdp", axis=0, tiled=True),
        lax.all_gather(second_shift, "fsdp", axis=0, tiled=True),
        lax.all_gather(cross_query_weight, "fsdp", axis=0, tiled=True),
        lax.all_gather(cross_query_bias, "fsdp", axis=0, tiled=True),
        lax.all_gather(cross_key_weight, "fsdp", axis=0, tiled=True),
        lax.all_gather(cross_value_weight, "fsdp", axis=0, tiled=True),
        lax.all_gather(cross_value_bias, "fsdp", axis=0, tiled=True),
        lax.all_gather(cross_out_weight, "fsdp", axis=0, tiled=True),
        lax.all_gather(cross_out_bias, "fsdp", axis=0, tiled=True),
        lax.all_gather(third_gain, "fsdp", axis=0, tiled=True),
        lax.all_gather(third_shift, "fsdp", axis=0, tiled=True),
        lax.all_gather(expand_weight, "fsdp", axis=0, tiled=True),
        lax.all_gather(expand_bias, "fsdp", axis=0, tiled=True),
        lax.all_gather(reduce_weight, "fsdp", axis=0, tiled=True),
        lax.all_gather(reduce_bias, "fsdp", axis=0, tiled=True),
    )
    (
        gain_one,
        shift_one,
        query_mat,
        query_add,
        key_mat,
        value_mat,
        value_add,
        self_out_mat,
        self_out_add,
        gain_two,
        shift_two,
        cross_query_mat,
        cross_query_add,
        cross_key_mat,
        cross_value_mat,
        cross_value_add,
        cross_out_mat,
        cross_output_bias_term,
        gain_three,
        third_norm_shift,
        expand_mat,
        expand_add,
        reduce_mat,
        reduce_add,
    ) = gathered
    slot_count, local_len, model_width = tokens.shape
    total_len = local_len * lax.axis_size("ctx")
    block_rows = math.gcd(local_len, 512)
    block_count = total_len // block_rows
    own_pos = lax.axis_index("ctx") * local_len + jnp.arange(local_len, dtype=jnp.int32)
    valid_rows = (own_pos[None, :] < lengths[:, None]).astype(jnp.float32)[:, :, None]
    residual = tokens.astype(jnp.float32)
    normed_one, norm_back_one = jax.vjp(
        layer_norm, residual, gain_one.astype(jnp.float32), shift_one.astype(jnp.float32)
    )
    normed_one = normed_one.astype(jnp.bfloat16)
    query_rows = (forward_mult(normed_one, query_mat) + query_add.astype(jnp.float32)).astype(
        jnp.bfloat16
    )
    key_rows = forward_mult(normed_one, key_mat).astype(jnp.bfloat16)
    value_rows = (forward_mult(normed_one, value_mat) + value_add.astype(jnp.float32)).astype(
        jnp.bfloat16
    )
    start_carry = (
        jnp.zeros((slot_count, local_len, HEADS, HEAD_DIM), jnp.float32),
        jnp.full((slot_count, HEADS, local_len), masked, jnp.float32),
        jnp.zeros((slot_count, HEADS, local_len), jnp.float32),
    )
    pieces = (
        lax.all_gather(key_rows, "ctx", axis=1, tiled=True),
        lax.all_gather(value_rows, "ctx", axis=1, tiled=True),
    )
    piece_rows = pieces[0].shape[1]
    inner_rows = math.gcd(piece_rows, 512)

    def inner_step(inner_index, fold_state):
        block_begin = inner_index * inner_rows
        key_block = lax.dynamic_slice_in_dim(pieces[0], block_begin, inner_rows, 1)
        value_block = lax.dynamic_slice_in_dim(pieces[1], block_begin, inner_rows, 1)
        key_pos = block_begin + jnp.arange(inner_rows, dtype=jnp.int32)
        return fold_update(
            fold_state, key_block, value_block, query_rows, own_pos, key_pos, lengths
        )

    running, row_top, row_total = lax.fori_loop(
        0, piece_rows // inner_rows, inner_step, start_carry
    )
    mixed_full = merge_heads(running / jnp.swapaxes(row_total, 1, 2)[..., None])
    mixed_rows = mixed_full.astype(jnp.bfloat16)
    row_lse = row_top + jnp.log(row_total)
    after_self = (
        residual + forward_mult(mixed_rows, self_out_mat) + self_out_add.astype(jnp.float32)
    )
    normed_two, norm_back_two = jax.vjp(
        layer_norm, after_self, gain_two.astype(jnp.float32), shift_two.astype(jnp.float32)
    )
    normed_two = normed_two.astype(jnp.bfloat16)
    cross_query = (
        forward_mult(normed_two, cross_query_mat) + cross_query_add.astype(jnp.float32)
    ).astype(jnp.bfloat16)
    cross_keys = forward_mult(encoder_states, cross_key_mat).astype(jnp.bfloat16)
    cross_values = (
        forward_mult(encoder_states, cross_value_mat) + cross_value_add.astype(jnp.float32)
    ).astype(jnp.bfloat16)
    cross_rows = lax.map(cross_attention_forward, (cross_query, cross_keys, cross_values)).astype(
        jnp.bfloat16
    )
    after_cross = (
        after_self
        + forward_mult(cross_rows, cross_out_mat)
        + cross_output_bias_term.astype(jnp.float32)
    )
    normed_three, norm_back_three = jax.vjp(
        layer_norm,
        after_cross,
        gain_three.astype(jnp.float32),
        third_norm_shift.astype(jnp.float32),
    )
    normed_three = normed_three.astype(jnp.bfloat16)
    expanded = forward_mult(normed_three, expand_mat) + expand_add.astype(jnp.float32)
    activated, gelu_back = jax.vjp(gelu_exact, expanded)
    activated = activated.astype(jnp.bfloat16)
    layer_out = (
        after_cross + forward_mult(activated, reduce_mat) + reduce_add.astype(jnp.float32)
    ) * valid_rows
    incoming_gradient = cotangent.astype(jnp.float32) * valid_rows
    reduce_up = incoming_gradient.astype(jnp.bfloat16)
    gradient_reduce = weight_grad(activated, reduce_up)
    gradient_reduce_add = bias_grad(reduce_up)
    expand_up = gelu_back(backward_product(reduce_up, reduce_mat))[0].astype(jnp.bfloat16)
    gradient_expand = weight_grad(normed_three, expand_up)
    gradient_expand_add = bias_grad(expand_up)
    input_part, gradient_gain_three, gradient_shift_three = norm_back_three(
        backward_product(expand_up, expand_mat)
    )
    incoming_gradient = incoming_gradient + input_part
    cross_out_up = incoming_gradient.astype(jnp.bfloat16)
    gradient_cross_out = weight_grad(cross_rows, cross_out_up)
    gradient_cross_out_add = bias_grad(cross_out_up)
    cross_dout = backward_product(cross_out_up, cross_out_mat).astype(jnp.bfloat16)
    cross_query_part, cross_key_part, cross_value_part = lax.map(
        cross_backward, (cross_query, cross_keys, cross_values, cross_dout)
    )
    cross_key_sum, cross_value_sum = (
        lax.psum(cross_key_part.astype(jnp.bfloat16), "ctx").astype(jnp.float32),
        lax.psum(cross_value_part.astype(jnp.bfloat16), "ctx").astype(jnp.float32),
    )
    cross_key_up = cross_key_sum.astype(jnp.bfloat16)
    cross_value_up = cross_value_sum.astype(jnp.bfloat16)
    cross_query_up = cross_query_part.astype(jnp.bfloat16)
    gradient_cross_query = weight_grad(normed_two, cross_query_up)
    gradient_cross_query_add = bias_grad(cross_query_up)
    gradient_cross_key = weight_grad(encoder_states, cross_key_up)
    gradient_cross_value = weight_grad(encoder_states, cross_value_up)
    gradient_cross_value_add = bias_grad(cross_value_up)
    encoder_grads = backward_product(cross_key_up, cross_key_mat) + backward_product(
        cross_value_up, cross_value_mat
    )
    input_part, gradient_gain_two, gradient_shift_two = norm_back_two(
        backward_product(cross_query_up, cross_query_mat)
    )
    incoming_gradient = incoming_gradient + input_part
    self_out_up = incoming_gradient.astype(jnp.bfloat16)
    gradient_self_out = weight_grad(mixed_rows, self_out_up)
    gradient_self_out_add = bias_grad(self_out_up)
    dout_rows = backward_product(self_out_up, self_out_mat).astype(jnp.bfloat16)
    row_delta = jnp.swapaxes(
        jnp.sum(split_heads(dout_rows.astype(jnp.float32)) * split_heads(mixed_full), axis=-1), 1, 2
    )
    zero_rows = jnp.zeros((slot_count, local_len, model_width), jnp.float32)
    block_indices = jnp.arange(block_count, dtype=jnp.int32)
    all_keys, all_values = (
        lax.all_gather(key_rows, "ctx", axis=1, tiled=True),
        lax.all_gather(value_rows, "ctx", axis=1, tiled=True),
    )

    def key_step(query_sum, block_index):
        block_begin = block_index * block_rows
        key_block = lax.dynamic_slice_in_dim(all_keys, block_begin, block_rows, 1)
        value_block = lax.dynamic_slice_in_dim(all_values, block_begin, block_rows, 1)
        key_pos = block_begin + jnp.arange(block_rows, dtype=jnp.int32)
        allowed = allowed_mask(own_pos, key_pos, lengths)
        query_part, key_part, value_part = tile_grads(
            query_rows, dout_rows, row_lse, row_delta, key_block, value_block, allowed
        )
        return (query_sum + query_part, (key_part, value_part))

    query_sum, (key_blocks, value_blocks) = lax.scan(key_step, zero_rows, block_indices)
    key_own, value_own = (
        lax.psum_scatter(
            key_blocks.astype(jnp.bfloat16), "ctx", scatter_dimension=0, tiled=True
        ).astype(jnp.float32),
        lax.psum_scatter(
            value_blocks.astype(jnp.bfloat16), "ctx", scatter_dimension=0, tiled=True
        ).astype(jnp.float32),
    )
    query_up = query_sum.astype(jnp.bfloat16)
    key_up = regroup_rows(key_own).astype(jnp.bfloat16)
    value_up = regroup_rows(value_own).astype(jnp.bfloat16)
    gradient_query = weight_grad(normed_one, query_up)
    gradient_query_add = bias_grad(query_up)
    gradient_key = weight_grad(normed_one, key_up)
    gradient_value = weight_grad(normed_one, value_up)
    gradient_value_add = bias_grad(value_up)
    normed_up = (
        backward_product(query_up, query_mat)
        + backward_product(key_up, key_mat)
        + backward_product(value_up, value_mat)
    )
    input_part, gradient_gain_one, gradient_shift_one = norm_back_one(normed_up)
    token_grads = incoming_gradient + input_part
    shards = (
        lax.psum_scatter(
            gradient_gain_one.astype(jnp.bfloat16), "fsdp", scatter_dimension=0, tiled=True
        ).astype(jnp.float32),
        lax.psum_scatter(
            gradient_shift_one.astype(jnp.bfloat16), "fsdp", scatter_dimension=0, tiled=True
        ).astype(jnp.float32),
        lax.psum_scatter(
            gradient_query.astype(jnp.bfloat16), "fsdp", scatter_dimension=0, tiled=True
        ).astype(jnp.float32),
        lax.psum_scatter(
            gradient_query_add.astype(jnp.bfloat16), "fsdp", scatter_dimension=0, tiled=True
        ).astype(jnp.float32),
        lax.psum_scatter(
            gradient_key.astype(jnp.bfloat16), "fsdp", scatter_dimension=0, tiled=True
        ).astype(jnp.float32),
        lax.psum_scatter(
            gradient_value.astype(jnp.bfloat16), "fsdp", scatter_dimension=0, tiled=True
        ).astype(jnp.float32),
        lax.psum_scatter(
            gradient_value_add.astype(jnp.bfloat16), "fsdp", scatter_dimension=0, tiled=True
        ).astype(jnp.float32),
        lax.psum_scatter(
            gradient_self_out.astype(jnp.bfloat16), "fsdp", scatter_dimension=0, tiled=True
        ).astype(jnp.float32),
        lax.psum_scatter(
            gradient_self_out_add.astype(jnp.bfloat16), "fsdp", scatter_dimension=0, tiled=True
        ).astype(jnp.float32),
        lax.psum_scatter(
            gradient_gain_two.astype(jnp.bfloat16), "fsdp", scatter_dimension=0, tiled=True
        ).astype(jnp.float32),
        lax.psum_scatter(
            gradient_shift_two.astype(jnp.bfloat16), "fsdp", scatter_dimension=0, tiled=True
        ).astype(jnp.float32),
        lax.psum_scatter(
            gradient_cross_query.astype(jnp.bfloat16), "fsdp", scatter_dimension=0, tiled=True
        ).astype(jnp.float32),
        lax.psum_scatter(
            gradient_cross_query_add.astype(jnp.bfloat16), "fsdp", scatter_dimension=0, tiled=True
        ).astype(jnp.float32),
        lax.psum_scatter(
            gradient_cross_key.astype(jnp.bfloat16), "fsdp", scatter_dimension=0, tiled=True
        ).astype(jnp.float32),
        lax.psum_scatter(
            gradient_cross_value.astype(jnp.bfloat16), "fsdp", scatter_dimension=0, tiled=True
        ).astype(jnp.float32),
        lax.psum_scatter(
            gradient_cross_value_add.astype(jnp.bfloat16), "fsdp", scatter_dimension=0, tiled=True
        ).astype(jnp.float32),
        lax.psum_scatter(
            gradient_cross_out.astype(jnp.bfloat16), "fsdp", scatter_dimension=0, tiled=True
        ).astype(jnp.float32),
        lax.psum_scatter(
            gradient_cross_out_add.astype(jnp.bfloat16), "fsdp", scatter_dimension=0, tiled=True
        ).astype(jnp.float32),
        lax.psum_scatter(
            gradient_gain_three.astype(jnp.bfloat16), "fsdp", scatter_dimension=0, tiled=True
        ).astype(jnp.float32),
        lax.psum_scatter(
            gradient_shift_three.astype(jnp.bfloat16), "fsdp", scatter_dimension=0, tiled=True
        ).astype(jnp.float32),
        lax.psum_scatter(
            gradient_expand.astype(jnp.bfloat16), "fsdp", scatter_dimension=0, tiled=True
        ).astype(jnp.float32),
        lax.psum_scatter(
            gradient_expand_add.astype(jnp.bfloat16), "fsdp", scatter_dimension=0, tiled=True
        ).astype(jnp.float32),
        lax.psum_scatter(
            gradient_reduce.astype(jnp.bfloat16), "fsdp", scatter_dimension=0, tiled=True
        ).astype(jnp.float32),
        lax.psum_scatter(
            gradient_reduce_add.astype(jnp.bfloat16), "fsdp", scatter_dimension=0, tiled=True
        ).astype(jnp.float32),
    )
    summed = (
        lax.psum(shards[0].astype(jnp.bfloat16), "ctx").astype(jnp.float32),
        lax.psum(shards[1].astype(jnp.bfloat16), "ctx").astype(jnp.float32),
        lax.psum(shards[2].astype(jnp.bfloat16), "ctx").astype(jnp.float32),
        lax.psum(shards[3].astype(jnp.bfloat16), "ctx").astype(jnp.float32),
        lax.psum(shards[4].astype(jnp.bfloat16), "ctx").astype(jnp.float32),
        lax.psum(shards[5].astype(jnp.bfloat16), "ctx").astype(jnp.float32),
        lax.psum(shards[6].astype(jnp.bfloat16), "ctx").astype(jnp.float32),
        lax.psum(shards[7].astype(jnp.bfloat16), "ctx").astype(jnp.float32),
        lax.psum(shards[8].astype(jnp.bfloat16), "ctx").astype(jnp.float32),
        lax.psum(shards[9].astype(jnp.bfloat16), "ctx").astype(jnp.float32),
        lax.psum(shards[10].astype(jnp.bfloat16), "ctx").astype(jnp.float32),
        lax.psum(shards[11].astype(jnp.bfloat16), "ctx").astype(jnp.float32),
        lax.psum(shards[12].astype(jnp.bfloat16), "ctx").astype(jnp.float32),
        lax.psum(shards[16].astype(jnp.bfloat16), "ctx").astype(jnp.float32),
        lax.psum(shards[17].astype(jnp.bfloat16), "ctx").astype(jnp.float32),
        lax.psum(shards[18].astype(jnp.bfloat16), "ctx").astype(jnp.float32),
        lax.psum(shards[19].astype(jnp.bfloat16), "ctx").astype(jnp.float32),
        lax.psum(shards[20].astype(jnp.bfloat16), "ctx").astype(jnp.float32),
        lax.psum(shards[21].astype(jnp.bfloat16), "ctx").astype(jnp.float32),
        lax.psum(shards[22].astype(jnp.bfloat16), "ctx").astype(jnp.float32),
        lax.psum(shards[23].astype(jnp.bfloat16), "ctx").astype(jnp.float32),
    )
    return (
        layer_out,
        token_grads,
        encoder_grads,
        summed[0],
        summed[1],
        summed[2],
        summed[3],
        summed[4],
        summed[5],
        summed[6],
        summed[7],
        summed[8],
        summed[9],
        summed[10],
        summed[11],
        summed[12],
        shards[13],
        shards[14],
        shards[15],
        summed[13],
        summed[14],
        summed[15],
        summed[16],
        summed[17],
        summed[18],
        summed[19],
        summed[20],
    )


def solution(mesh):
    placed = (
        P("fsdp", "ctx", None),
        P("fsdp", None, None),
        P("fsdp"),
        P("fsdp", "ctx", None),
        P("fsdp"),
        P("fsdp"),
        P("fsdp", None),
        P("fsdp"),
        P("fsdp", None),
        P("fsdp", None),
        P("fsdp"),
        P("fsdp", None),
        P("fsdp"),
        P("fsdp"),
        P("fsdp"),
        P("fsdp", None),
        P("fsdp"),
        P("fsdp", None),
        P("fsdp", None),
        P("fsdp"),
        P("fsdp", None),
        P("fsdp"),
        P("fsdp"),
        P("fsdp"),
        P("fsdp", None),
        P("fsdp"),
        P("fsdp", None),
        P("fsdp"),
    )
    return jax.shard_map(
        body,
        mesh=mesh,
        in_specs=placed,
        out_specs=(
            P("fsdp", "ctx", None),
            P("fsdp", "ctx", None),
            P("fsdp", None, None),
            P("fsdp"),
            P("fsdp"),
            P("fsdp", None),
            P("fsdp"),
            P("fsdp", None),
            P("fsdp", None),
            P("fsdp"),
            P("fsdp", None),
            P("fsdp"),
            P("fsdp"),
            P("fsdp"),
            P("fsdp", None),
            P("fsdp"),
            P("fsdp", None),
            P("fsdp", None),
            P("fsdp"),
            P("fsdp", None),
            P("fsdp"),
            P("fsdp"),
            P("fsdp"),
            P("fsdp", None),
            P("fsdp"),
            P("fsdp", None),
            P("fsdp"),
        ),
        check_vma=False,
    )
```

profile of v0, /device:TPU:0, one launch (start us, length us, event | category | flops | bytes accessed | tf_op | source)
XLA Modules:
  0.0 1703.2 jit_solution(16578451521351670025)
XLA Ops:
  20.9 18.4 %all-reduce.30 = (bf16[768]{0:T(1024)(128)(2,1)S(1)}, bf16[768]{0:T(1024)(128)(2,1)S(1)}, bf16[768]{0:T(1024)(128)(2,1)S(1)}, bf16[768]{0:T(1024)(128)(2,1)S(1)}...) all-reduce(bf16[768]{0:T(1024)(128)(2,1)S(1)} %dynamic-update-slice, ...), channel_id=1, replica_groups=mesh['ctx'=8,'fsdp'=4] {'fsdp'}, use_global_device_ids=true, to_apply=%add.8 | all-reduce | flops 9216 | bytes 36864
  43.8 26.3 %all-gather.16.cloned.1.call-done = bf16[768,768]{1,0:T(8,128)(2,1)} async-done(((bf16[192,768]{1,0:T(8,128)(2,1)}), bf16[768,768]{1,0:T(8,128)(2,1)}) %all-gather.16.cloned.1.call-update) | async-done | bytes 1179664 | tf_op jit(solution)/shard_map/all_gather | solution.py:222
  104.0 24.8 %all-gather.28.cloned.1.call-done = bf16[768,768]{1,0:T(8,128)(2,1)} async-done(((bf16[192,768]{1,0:T(8,128)(2,1)}), bf16[768,768]{1,0:T(8,128)(2,1)}) %all-gather.28.cloned.1.call-update) | async-done | bytes 1179664 | tf_op jit(solution)/shard_map/all_gather | solution.py:231
  137.9 20.2 %all-gather.24.cloned.1.call-done = bf16[768,768]{1,0:T(8,128)(2,1)} async-done(((bf16[192,768]{1,0:T(8,128)(2,1)}), bf16[768,768]{1,0:T(8,128)(2,1)}) %all-gather.24.cloned.1.call-update) | async-done | bytes 1179664 | tf_op jit(solution)/shard_map/all_gather | solution.py:232
  167.0 57.3 %all-gather.38.cloned.1.call-done = bf16[4096,768]{1,0:T(8,128)(2,1)} async-done(((bf16[512,768]{1,0:T(8,128)(2,1)}), bf16[4096,768]{1,0:T(8,128)(2,1)}) %all-gather.38.cloned.1.call-update) | async-done | bytes 6291472 | tf_op jit(solution)/shard_map/all_gather | solution.py:294
  233.0 57.0 %all-gather.36.cloned.1.call-done = bf16[4096,768]{1,0:T(8,128)(2,1)} async-done(((bf16[512,768]{1,0:T(8,128)(2,1)}), bf16[4096,768]{1,0:T(8,128)(2,1)}) %all-gather.36.cloned.1.call-update) | async-done | bytes 6291472 | tf_op jit(solution)/shard_map/all_gather | solution.py:293
  298.7 187.2 %while.9 = (s32[]{:T(128)}, f32[1,512,12,64]{1,3,2,0:T(8,128)}, f32[1,12,512]{2,1,0:T(8,128)S(1)}, f32[1,12,512]{2,1,0:T(8,128)S(1)}, s32[1]{0:T(128)}, /*index=...) while((s32[]{:T(128)}, f32[1,512,12,64]{1,3,2,0:T(8,128)}, ...), condition=%wide.region_5.6_spmd.clone, body=%wide.region_2.5_spmd.clone.sunk | while | flops 841652224 | bytes 98182368 | solution.py:308
  498.9 20.7 %fusion.145 = (f32[12,512]{1,0:T(8,128)S(1)}, f32[12,512,1500]{1,2,0:T(8,128)}) fusion(bf16[512,12,64]{0,2,1:T(8,128)(2,1)S(1)} %bitcast.388, bf16[1500,12,64]{0,2,1:T(8,128)(2,1)} %bitcast.383), kind=kOutput, calls=%fused_computation.207 | convolution fusion | flops 1207297536 | bytes 39979008 | tf_op jit(solution)/shard_map/while/body/eval_jaxpr/sub | solution.py:139
  538.2 21.1 %multiply_convert_fusion.1 = (bf16[512,3072]{1,0:T(8,128)(2,1)}, f32[512,3072]{1,0:T(8,128)}, f32[512,3072]{1,0:T(8,128)}) fusion(f32[3072]{0:T(1024)S(1)} %bitcast.408, bf16[768,3072]{1,0:T(8,128)(2,1)} %all-gather.32.cloned.1.call-done, f32[1,512,768]{2,1,0:T(8,128)} %copy-done.9, f32[768]{0:T(1024)S(1)} %convert_element_type.480, ...), kind=kOutput, calls=%fused_computation.60 | convolution fusion | flops 2521694208 | bytes 22042624 | tf_op jit(solution)/shard_map/vrw,wk->vrk/dot_general | solution.py:36
  579.3 28.1 %multiply_reduce_fusion = (f32[12,512]{1,0:T(8,128)S(1)}, f32[12,512,1500]{1,2,0:T(8,128)}) fusion(f32[12,512,1500]{1,2,0:T(8,128)} %get-tuple-element.648, f32[12,512]{1,0:T(8,128)S(1)} %get-tuple-element.647, bf16[512,12,64]{0,2,1:T(8,128)(2,1)} %bitcast.400, bf16[1500,12,64]{0,2,1:T(8,128)(2,1)} %bitcast.394), kind=kOutput, calls=%fused_computation.47 | convolution fusion | flops 1207289856 | bytes 76867584 | tf_op jit(solution)/shard_map/while/body/eval_jaxpr/qhe,khe->hqk/dot_general | solution.py:171
  607.4 30.7 %multiply_convert_fusion = bf16[12,512,1500]{1,2,0:T(8,128)(2,1)} fusion(f32[12,512,1500]{1,2,0:T(8,128)} %get-tuple-element.654, f32[12,512]{1,0:T(8,128)S(1)} %get-tuple-element.653, f32[12,512,1500]{1,2,0:T(8,128)} %get-tuple-element.648, f32[12,512]{1,0:T(8,128)S(1)} %get-tuple-element.647), kind=kLoop, calls=%fused_computation.46 | loop fusion | flops 36864000 | bytes 92209152 | tf_op jit(solution)/shard_map/while/body/eval_jaxpr/convert_element_type | solution.py:175
  662.1 272.5 %while.10 = (s32[]{:T(128)}, f32[1,512,768]{1,2,0:T(8,128)}, bf16[8,1,512,768]{2,3,1,0:T(8,128)(2,1)}, bf16[8,1,512,768]{2,3,1,0:T(8,128)(2,1)}, s32[8]{0:T(128)...) while((s32[]{:T(128)}, f32[1,512,768]{1,2,0:T(8,128)}, ...), condition=%wide.region_19.20_spmd.clone, body=%wide.region_18.19_spmd.clone.sunk | while | flops 2047215616 | bytes 80299792 | solution.py:411
  965.0 38.1 %reduce-scatter.17.cloned.1.call-done = bf16[1,1,512,768]{2,3,1,0:T(8,128)(2,1)} async-done(((bf16[8,1,512,768]{2,3,1,0:T(8,128)(2,1)}), bf16[1,1,512,768]{2,3,1,0:T(8,128)(2,1)}) %reduce-scatter.17.cloned.1.call-update) | async-done | bytes 786448 | tf_op jit(solution)/shard_map/reduce_scatter | solution.py:413
  1006.4 67.1 %reduce-scatter.19.cloned.1.call-done = bf16[1,1,512,768]{2,3,1,0:T(8,128)(2,1)} async-done(((bf16[8,1,512,768]{2,3,1,0:T(8,128)(2,1)}), bf16[1,1,512,768]{2,3,1,0:T(8,128)(2,1)}) %reduce-scatter.19.cloned.1.call-update) | async-done | bytes 786448 | tf_op jit(solution)/shard_map/reduce_scatter | solution.py:416
  1104.4 30.6 %reduce-scatter.27.cloned.1.call-done = bf16[192,768]{1,0:T(8,128)(2,1)} async-done(((bf16[768,768]{1,0:T(8,128)(2,1)}), bf16[192,768]{1,0:T(8,128)(2,1)}) %reduce-scatter.27.cloned.1.call-update) | async-done | bytes 294928 | tf_op jit(solution)/shard_map/reduce_scatter | solution.py:457
  1135.0 32.1 %reduce-scatter.21.cloned.1.call-done = bf16[192,768]{1,0:T(8,128)(2,1)} async-done(((bf16[768,768]{1,0:T(8,128)(2,1)}), bf16[192,768]{1,0:T(8,128)(2,1)}) %reduce-scatter.21.cloned.1.call-update) | async-done | bytes 294928 | tf_op jit(solution)/shard_map/reduce_scatter | solution.py:442
  1167.1 31.5 %reduce-scatter.31.cloned.1.call-done = bf16[192,768]{1,0:T(8,128)(2,1)} async-done(((bf16[768,768]{1,0:T(8,128)(2,1)}), bf16[192,768]{1,0:T(8,128)(2,1)}) %reduce-scatter.31.cloned.1.call-update) | async-done | bytes 294928 | tf_op jit(solution)/shard_map/reduce_scatter | solution.py:484
  1198.6 60.0 %reduce-scatter.33.cloned.1.call-done = bf16[192,3072]{1,0:T(8,128)(2,1)} async-done(((bf16[768,3072]{1,0:T(8,128)(2,1)}), bf16[192,3072]{1,0:T(8,128)(2,1)}) %reduce-scatter.33.cloned.1.call-update) | async-done | bytes 1179664 | tf_op jit(solution)/shard_map/reduce_scatter | solution.py:496
  1258.6 59.8 %reduce-scatter.35.cloned.1.call-done = bf16[768,768]{1,0:T(8,128)(2,1)} async-done(((bf16[3072,768]{1,0:T(8,128)(2,1)}), bf16[768,768]{1,0:T(8,128)(2,1)}) %reduce-scatter.35.cloned.1.call-update) | async-done | bytes 1179664 | tf_op jit(solution)/shard_map/reduce_scatter | solution.py:502
  1318.4 32.2 %reduce-scatter.23.cloned.1.call-done = bf16[192,768]{1,0:T(8,128)(2,1)} async-done(((bf16[768,768]{1,0:T(8,128)(2,1)}), bf16[192,768]{1,0:T(8,128)(2,1)}) %reduce-scatter.23.cloned.1.call-update) | async-done | bytes 294928 | tf_op jit(solution)/shard_map/reduce_scatter | solution.py:448
  1350.6 32.2 %reduce-scatter.25.cloned.1.call-done = bf16[192,768]{1,0:T(8,128)(2,1)} async-done(((bf16[768,768]{1,0:T(8,128)(2,1)}), bf16[192,768]{1,0:T(8,128)(2,1)}) %reduce-scatter.25.cloned.1.call-update) | async-done | bytes 294928 | tf_op jit(solution)/shard_map/reduce_scatter | solution.py:451
  1384.5 187.2 %all-reduce.33.cloned.1.call-done = (bf16[1500,768]{0,1:T(8,128)(2,1)}, bf16[1,1500,768]{1,2,0:T(8,128)(2,1)}, bf16[192,768]{1,0:T(8,128)(2,1)}, bf16[192,768]{1...) async-done(((bf16[1500,768]{0,1:T(8,128)(2,1)}, ...) | async-done | bytes 8736784 | tf_op jit(solution)/shard_map/psum | solution.py:368
  1607.0 17.4 %all-reduce.29 = (bf16[768]{0:T(1024)(128)(2,1)S(1)}, bf16[768]{0:T(1024)(128)(2,1)S(1)}, bf16[768]{0:T(1024)(128)(2,1)S(1)}, bf16[768]{0:T(1024)(128)(2,1)S(1)}...) all-reduce(bf16[768]{0:T(1024)(128)(2,1)S(1)} %dynamic-update-slice, ...), channel_id=1, replica_groups=mesh['ctx'=8,'fsdp'=4] {'fsdp'}, use_global_device_ids=true, to_apply=%add.12 | all-reduce | flops 13824 | bytes 55296
  1653.3 25.8 %copy.113 = f32[1,1500,768]{2,0,1:T(1,128)} copy(f32[1,1500,768]{2,1,0:T(8,128)S(1)} %add_bitcast_fusion) | data formatting | bytes 9216000
  (636 shorter events, 759.7 us)
Async XLA Ops:
  8.0 62.1 %all-gather.16.cloned.1.call-start = ((), (), s32[]{:S(2)}) async-start(), calls=%async_computation.12 | async-start | bytes 1474560 | tf_op jit(solution)/shard_map/all_gather | solution.py:222
  8.7 90.8 %all-gather.18.cloned.1.call-start = ((), (), s32[]{:S(2)}) async-start(), calls=%async_computation.13 | async-start | bytes 1474560 | tf_op jit(solution)/shard_map/all_gather | solution.py:220
  9.5 119.4 %all-gather.28.cloned.1.call-start = ((), (), s32[]{:S(2)}) async-start(), calls=%async_computation.18 | async-start | bytes 1474560 | tf_op jit(solution)/shard_map/all_gather | solution.py:231
  10.1 148.1 %all-gather.24.cloned.1.call-start = ((), (), s32[]{:S(2)}) async-start(), calls=%async_computation.16 | async-start | bytes 1474560 | tf_op jit(solution)/shard_map/all_gather | solution.py:232
  10.6 213.7 %all-gather.38.cloned.1.call-start = ((), (), s32[]{:S(2)}) async-start(), calls=%async_computation.33 | async-start | bytes 7077888 | tf_op jit(solution)/shard_map/all_gather | solution.py:294
  43.7 246.2 %all-gather.36.cloned.1.call-start = ((), (), s32[]{:S(2)}) async-start(), calls=%async_computation.32 | async-start | bytes 7077888 | tf_op jit(solution)/shard_map/all_gather | solution.py:293
  73.2 415.6 %all-gather.22.cloned.1.call-start = ((), (), s32[]{:S(2)}) async-start(), calls=%async_computation.15 | async-start | bytes 1474560 | tf_op jit(solution)/shard_map/all_gather | solution.py:225
  73.9 419.5 %all-gather.26.cloned.1.call-start = ((), (), s32[]{:S(2)}) async-start(), calls=%async_computation.17 | async-start | bytes 1474560 | tf_op jit(solution)/shard_map/all_gather | solution.py:229
  74.7 459.0 %all-gather.30.cloned.1.call-start = ((), (), s32[]{:S(2)}) async-start(), calls=%async_computation.19 | async-start | bytes 1474560 | tf_op jit(solution)/shard_map/all_gather | solution.py:234
  75.2 462.9 %all-gather.32.cloned.1.call-start = ((), (), s32[]{:S(2)}) async-start(), calls=%async_computation.20 | async-start | bytes 5898240 | tf_op jit(solution)/shard_map/all_gather | solution.py:238
  76.0 483.3 %all-gather.34.cloned.1.call-start = ((), (), s32[]{:S(2)}) async-start(), calls=%async_computation.21 | async-start | bytes 5898240 | tf_op jit(solution)/shard_map/all_gather | solution.py:240
  76.5 926.6 %reduce-scatter.17.cloned.1.call-start = ((), (), s32[]{:S(2)}) async-start(), calls=%async_computation.22 | async-start | bytes 7077888 | tf_op jit(solution)/shard_map/reduce_scatter | solution.py:413
  934.7 138.8 %reduce-scatter.19.cloned.1.call-start = ((), (), s32[]{:S(2)}) async-start(), calls=%async_computation.23 | async-start | bytes 7077888 | tf_op jit(solution)/shard_map/reduce_scatter | solution.py:416
  935.2 169.2 %reduce-scatter.29.cloned.1.call-start = ((), (), s32[]{:S(2)}) async-start(), calls=%async_computation.28 | async-start | bytes 1474560 | tf_op jit(solution)/shard_map/reduce_scatter | solution.py:469
  939.4 195.6 %reduce-scatter.27.cloned.1.call-start = ((), (), s32[]{:S(2)}) async-start(), calls=%async_computation.27 | async-start | bytes 1474560 | tf_op jit(solution)/shard_map/reduce_scatter | solution.py:457
  943.1 224.0 %reduce-scatter.21.cloned.1.call-start = ((), (), s32[]{:S(2)}) async-start(), calls=%async_computation.24 | async-start | bytes 1474560 | tf_op jit(solution)/shard_map/reduce_scatter | solution.py:442
  946.8 251.8 %reduce-scatter.31.cloned.1.call-start = ((), (), s32[]{:S(2)}) async-start(), calls=%async_computation.29 | async-start | bytes 1474560 | tf_op jit(solution)/shard_map/reduce_scatter | solution.py:484
  950.2 308.4 %reduce-scatter.33.cloned.1.call-start = ((), (), s32[]{:S(2)}) async-start(), calls=%async_computation.30 | async-start | bytes 5898240 | tf_op jit(solution)/shard_map/reduce_scatter | solution.py:496
  957.9 360.6 %reduce-scatter.35.cloned.1.call-start = ((), (), s32[]{:S(2)}) async-start(), calls=%async_computation.31 | async-start | bytes 5898240 | tf_op jit(solution)/shard_map/reduce_scatter | solution.py:502
  965.0 385.7 %reduce-scatter.23.cloned.1.call-start = ((), (), s32[]{:S(2)}) async-start(), calls=%async_computation.25 | async-start | bytes 1474560 | tf_op jit(solution)/shard_map/reduce_scatter | solution.py:448
  1006.4 376.5 %reduce-scatter.25.cloned.1.call-start = ((), (), s32[]{:S(2)}) async-start(), calls=%async_computation.26 | async-start | bytes 1474560 | tf_op jit(solution)/shard_map/reduce_scatter | solution.py:451
  1076.7 494.9 %all-reduce.33.cloned.1.call-start = ((), (), s32[]{:S(2)}) async-start(), calls=%async_computation.36 | async-start | bytes 17694720 | tf_op jit(solution)/shard_map/psum | solution.py:368
  1382.9 309.1 %reduce-scatter.37.cloned.1.call-start = ((), (), s32[]{:S(2)}) async-start(), calls=%async_computation.34 | async-start | bytes 1474560
  1578.7 115.4 %reduce-scatter.39.cloned.1.call-start = ((), (), s32[]{:S(2)}) async-start(), calls=%async_computation.35 | async-start | bytes 1474560
  (109 other events, 2964.5 us)
Sparse Core Ops, SparseCore 0:
  9.9 30.6 all-gather.19
  42.4 27.5 all-gather.15
  71.9 27.5 all-gather.17
  101.2 27.5 all-gather.27
  130.5 27.5 all-gather.23
  159.6 64.6 all-gather.37
  226.6 63.3 all-gather.35
  319.9 27.5 all-gather.25
  349.2 27.5 all-gather.29
  378.6 56.9 all-gather.31
  437.3 56.9 all-gather.33
  934.8 68.2 reduce-scatter.16
  1005.3 68.1 reduce-scatter.18
  1076.2 27.2 reduce-scatter.28
  1106.3 28.6 reduce-scatter.26
  1138.3 28.6 reduce-scatter.20
  1169.9 28.6 reduce-scatter.30
  1201.6 56.9 reduce-scatter.32
  1261.4 56.9 reduce-scatter.34
  1321.9 28.6 reduce-scatter.22
  1354.1 28.6 reduce-scatter.24
  1387.2 184.3 all-reduce.32
  1578.8 29.0 reduce-scatter.36
  1610.8 28.9 reduce-scatter.38
  (1 shorter events, 26.2 us)
where the time goes:
time: 1710 us; the launch traced here: 1700 us
  waiting for transfers between devices  777 us (45%)
  matrix products  517 us (30%)
  other arithmetic  173 us (10%)
  local copies, waits for them, and re-layouts  152 us (9%)
  blocking collectives  58.3 us (3%)
  between operations  18.5 us (1%)
    psum x1, waiting for transfers between devices, body(): lax.psum(cross_key_part.astype(jnp.bfloat16), 'ctx').astype(jnp.float32)  187 us
    unnamed x236, local copies, waits for them, and re-layouts  75.6 us
    reduce_scatter x1, waiting for transfers between devices, body(): lax.psum_scatter(value_blocks.astype(jnp.bfloat16), 'ctx', scatter_dimens...  67.1 us
    reduce_scatter x1, waiting for transfers between devices, body(): lax.psum_scatter(gradient_expand.astype(jnp.bfloat16), 'fsdp', scatter_di...  60 us
    reduce_scatter x1, waiting for transfers between devices, body(): lax.psum_scatter(gradient_reduce.astype(jnp.bfloat16), 'fsdp', scatter_di...  59.8 us
    reduce_sum x8, other arithmetic, fold_update(): row_total = row_total * factor + jnp.sum(weights, axis=-1)  58.5 us
    dot_general x8, matrix products, tile_grads(): jnp.einsum('shqk,sqhe->skhe', probability.astype(jnp.bfloat16), dout_head...  57.9 us
    all_gather x1, waiting for transfers between devices, body(): lax.all_gather(value_rows, 'ctx', axis=1, tiled=True)  57.3 us
  transfers between devices with their start and end apart: 25, of which 17 were waited for; matrix products, arithmetic and copies ran while one was open for 26% of the time, Pallas kernels for 0%

commit v1 on v0

v1 whole, which is shorter than its diff:
```python
import functools
import math

import jax
import jax.numpy as jnp
from jax import lax
from jax.experimental import pallas as pl
from jax.experimental.pallas import tpu as pltpu
from jax.sharding import Mesh
from jax.sharding import PartitionSpec as P

HEADS = 12
HEAD_DIM = 64
SCALE = HEAD_DIM ** (-0.5)
EPS = 1e-05
MASKED = -1e30
BF = jnp.bfloat16
F32 = jnp.float32


def cost(flops, nbytes, exps=0):
    return pl.CostEstimate(flops=int(flops), bytes_accessed=int(nbytes), transcendentals=int(exps))


def params(axes):
    return pltpu.CompilerParams(
        dimension_semantics=("arbitrary",) * axes, vmem_limit_bytes=60 * 1024 * 1024
    )


def masked_heads(flat, hg):
    zero = jnp.zeros((HEAD_DIM, flat.shape[1]), flat.dtype)
    out = []
    for h in range(hg):
        rows = [zero] * hg
        rows[h] = flat[h * HEAD_DIM : (h + 1) * HEAD_DIM]
        out.append(jnp.concatenate(rows, axis=0))
    return out


def tile_mask(block_pos, tile_start, shape, length, causal):
    key = tile_start + lax.broadcasted_iota(jnp.int32, shape, 0)
    inside = key < length
    if causal:
        query = block_pos + lax.broadcasted_iota(jnp.int32, shape, 1)
        inside = inside & (key <= query)
    return inside


def tile_bounds(base, qt, kt, length, causal, total):
    if causal:
        full = jnp.minimum(base, length) // kt
        end = (jnp.minimum(base + qt, length) + kt - 1) // kt
        return full, end
    return length // kt, (length + kt - 1) // kt


def fwd_kernel(hg, qt, kt, causal, rows_of, info, q_ref, k_ref, v_ref, o_ref, ob_ref, lse_ref,
               vt, qm, acc, mx, sm):
    block = pl.program_id(1)
    total = k_ref.shape[0]
    width = hg * HEAD_DIM

    @pl.when(block == 0)
    def _():
        vt[...] = v_ref[...].T

    flat = (q_ref[...] * BF(SCALE)).T
    for h, piece in enumerate(masked_heads(flat, hg)):
        qm[h] = piece
    acc[...] = jnp.zeros_like(acc)
    sm[...] = jnp.zeros_like(sm)
    mx[...] = jnp.full_like(mx, MASKED)
    base = rows_of(block, info)
    length = info[0]

    def step(j, masked):
        start = pl.multiple_of(j * kt, kt)
        keys = k_ref[pl.ds(start, kt), :]
        if masked:
            allowed = tile_mask(base, start, (kt, qt), length, causal)
        scores, tops = [], []
        for h in range(hg):
            s = jnp.dot(keys, qm[h], preferred_element_type=F32)
            if masked:
                s = jnp.where(allowed, s, MASKED)
            scores.append(s)
            tops.append(jnp.max(s, axis=0, keepdims=True))
        for h in range(hg):
            old = mx[h : h + 1, :]
            new = jnp.maximum(old, tops[h])
            p = jnp.exp(scores[h] - new)
            fix = jnp.exp(old - new)
            mx[h : h + 1, :] = new
            sm[h : h + 1, :] = sm[h : h + 1, :] * fix + jnp.sum(p, axis=0, keepdims=True)
            here = slice(h * HEAD_DIM, (h + 1) * HEAD_DIM)
            acc[here, :] = acc[here, :] * fix + jnp.dot(
                vt[here, pl.ds(start, kt)], p.astype(BF), preferred_element_type=F32
            )

    if causal:
        full, end = tile_bounds(base, qt, kt, length, causal, total)

        @pl.loop(0, full)
        def _(j):
            step(j, False)

        @pl.loop(full, end)
        def _(j):
            step(j, True)
    else:
        tiles = total // kt
        for j in range(tiles):
            step(j, j == tiles - 1)

    for h in range(hg):
        here = slice(h * HEAD_DIM, (h + 1) * HEAD_DIM)
        acc[here, :] = acc[here, :] / sm[h : h + 1, :]
    out = acc[...].T
    o_ref[...] = out
    ob_ref[...] = out.astype(BF)
    lse_ref[0, 0] = mx[:hg, :] + jnp.log(sm[:hg, :])


def bwd_kernel(hg, qt, kt, causal, rows_of, info, q_ref, do_ref, o_ref, lse_ref, k_ref, v_ref,
               dq_ref, dk_ref, dv_ref, kt_ref, qm, dm, qs, ds_, dk, dv, dqt, dl):
    block = pl.program_id(1)
    total = k_ref.shape[0]

    @pl.when(block == 0)
    def _():
        kt_ref[...] = k_ref[...].T
        dk[...] = jnp.zeros_like(dk)
        dv[...] = jnp.zeros_like(dv)

    q = q_ref[...] * BF(SCALE)
    do = do_ref[...]
    qflat = q.T
    dflat = do.T
    prod = (do.astype(F32) * o_ref[...]).T
    lane = lax.broadcasted_iota(jnp.int32, (qt, hg * HEAD_DIM), 1) // HEAD_DIM
    qpieces = masked_heads(qflat, hg)
    dpieces = masked_heads(dflat, hg)
    for h in range(hg):
        qm[h] = qpieces[h]
        dm[h] = dpieces[h]
        keep = lane == h
        qs[h * qt : (h + 1) * qt, :] = jnp.where(keep, q, jnp.zeros_like(q))
        ds_[h * qt : (h + 1) * qt, :] = jnp.where(keep, do, jnp.zeros_like(do))
        dl[h : h + 1, :] = jnp.sum(prod[h * HEAD_DIM : (h + 1) * HEAD_DIM], axis=0, keepdims=True)
    dqt[...] = jnp.zeros_like(dqt)
    base = rows_of(block, info)
    length = info[0]

    def step(j, masked):
        start = pl.multiple_of(j * kt, kt)
        keys = k_ref[pl.ds(start, kt), :]
        values = v_ref[pl.ds(start, kt), :]
        if masked:
            allowed = tile_mask(base, start, (kt, qt), length, causal)
        ps, gs = [], []
        for h in range(hg):
            s = jnp.dot(keys, qm[h], preferred_element_type=F32)
            p = jnp.exp(s - lse_ref[0, 0, h : h + 1, :])
            if masked:
                p = jnp.where(allowed, p, 0.0)
            dp = jnp.dot(values, dm[h], preferred_element_type=F32)
            g = (p * (dp - dl[h : h + 1, :])).astype(BF)
            ps.append(p.astype(BF))
            gs.append(g)
            here = slice(h * HEAD_DIM, (h + 1) * HEAD_DIM)
            dqt[here, :] += jnp.dot(kt_ref[here, pl.ds(start, kt)], g, preferred_element_type=F32)
        where = pl.ds(start, kt)
        dv[where, :] += jnp.dot(
            jnp.concatenate(ps, axis=1), ds_[...], preferred_element_type=F32
        )
        dk[where, :] += jnp.dot(
            jnp.concatenate(gs, axis=1), qs[...], preferred_element_type=F32
        )

    if causal:
        full, end = tile_bounds(base, qt, kt, length, causal, total)

        @pl.loop(0, full)
        def _(j):
            step(j, False)

        @pl.loop(full, end)
        def _(j):
            step(j, True)
    else:
        tiles = total // kt
        for j in range(tiles):
            step(j, j == tiles - 1)

    dq_ref[...] = (dqt[...] * SCALE).T.astype(BF)

    @pl.when(block == pl.num_programs(1) - 1)
    def _():
        dk_ref[...] = dk[...].astype(BF)
        dv_ref[...] = dv[...].astype(BF)


def flash_fwd(q, k, v, info, hg, qt, kt, causal, blocks, q_index, rows_of, name):
    total, all_width = k.shape
    width = hg * HEAD_DIM
    groups = all_width // width
    rows = blocks * qt
    pairs = rows * total * HEADS * (1 if not causal else 0.5) * groups * hg / HEADS
    return pl.pallas_call(
        functools.partial(fwd_kernel, hg, qt, kt, causal, rows_of),
        grid_spec=pltpu.PrefetchScalarGridSpec(
            num_scalar_prefetch=1,
            grid=(groups, blocks),
            in_specs=[
                pl.BlockSpec((qt, width), lambda g, i, s: (q_index(i, s), g)),
                pl.BlockSpec((total, width), lambda g, i, s: (0, g)),
                pl.BlockSpec((total, width), lambda g, i, s: (0, g)),
            ],
            out_specs=[
                pl.BlockSpec((qt, width), lambda g, i, s: (i, g)),
                pl.BlockSpec((qt, width), lambda g, i, s: (i, g)),
                pl.BlockSpec((1, 1, hg, qt), lambda g, i, s: (g, i, 0, 0)),
            ],
            scratch_shapes=[
                pltpu.VMEM((width, total), BF),
                pltpu.VMEM((hg, width, qt), BF),
                pltpu.VMEM((width, qt), F32),
                pltpu.VMEM((8, qt), F32),
                pltpu.VMEM((8, qt), F32),
            ],
        ),
        out_shape=[
            jax.ShapeDtypeStruct((rows, all_width), F32),
            jax.ShapeDtypeStruct((rows, all_width), BF),
            jax.ShapeDtypeStruct((groups, blocks, hg, qt), F32),
        ],
        compiler_params=params(2),
        cost_estimate=cost(pairs * 4 * 256, rows * all_width * 8 + total * all_width * 4, pairs),
        name=name,
    )(info, q, k, v)


def flash_bwd(q, do, o, lse, k, v, info, hg, qt, kt, causal, blocks, q_index, rows_of, name):
    total, all_width = k.shape
    width = hg * HEAD_DIM
    groups = all_width // width
    rows = blocks * qt
    pairs = rows * total * HEADS * (1 if not causal else 0.5) * groups * hg / HEADS
    return pl.pallas_call(
        functools.partial(bwd_kernel, hg, qt, kt, causal, rows_of),
        grid_spec=pltpu.PrefetchScalarGridSpec(
            num_scalar_prefetch=1,
            grid=(groups, blocks),
            in_specs=[
                pl.BlockSpec((qt, width), lambda g, i, s: (q_index(i, s), g)),
                pl.BlockSpec((qt, width), lambda g, i, s: (i, g)),
                pl.BlockSpec((qt, width), lambda g, i, s: (i, g)),
                pl.BlockSpec((1, 1, hg, qt), lambda g, i, s: (g, i, 0, 0)),
                pl.BlockSpec((total, width), lambda g, i, s: (0, g)),
                pl.BlockSpec((total, width), lambda g, i, s: (0, g)),
            ],
            out_specs=[
                pl.BlockSpec((qt, width), lambda g, i, s: (i, g)),
                pl.BlockSpec((total, width), lambda g, i, s: (0, g)),
                pl.BlockSpec((total, width), lambda g, i, s: (0, g)),
            ],
            scratch_shapes=[
                pltpu.VMEM((width, total), BF),
                pltpu.VMEM((hg, width, qt), BF),
                pltpu.VMEM((hg, width, qt), BF),
                pltpu.VMEM((hg * qt, width), BF),
                pltpu.VMEM((hg * qt, width), BF),
                pltpu.VMEM((total, width), F32),
                pltpu.VMEM((total, width), F32),
                pltpu.VMEM((width, qt), F32),
                pltpu.VMEM((8, qt), F32),
            ],
        ),
        out_shape=[
            jax.ShapeDtypeStruct((rows, all_width), BF),
            jax.ShapeDtypeStruct((total, all_width), BF),
            jax.ShapeDtypeStruct((total, all_width), BF),
        ],
        compiler_params=params(2),
        cost_estimate=cost(pairs * 10 * 256, rows * all_width * 10 + total * all_width * 8, pairs),
        name=name,
    )(info, q, do, o, lse, k, v)


def ln_qkv_kernel(x_ref, w_ref, add_ref, gain_ref, shift_ref, n_ref, q_ref, k_ref, v_ref):
    x = x_ref[...].astype(F32)
    centre = jnp.mean(x, axis=-1, keepdims=True)
    x = x - centre
    spread = jnp.mean(x * x, axis=-1, keepdims=True)
    n = (x * lax.rsqrt(spread + EPS) * gain_ref[...] + shift_ref[...]).astype(BF)
    n_ref[...] = n
    width = q_ref.shape[1]
    y = jnp.dot(n, w_ref[...], preferred_element_type=F32) + add_ref[...]
    y = y.astype(BF)
    q_ref[...] = y[:, :width]
    k_ref[...] = y[:, width : 2 * width]
    v_ref[...] = y[:, 2 * width :]


def ln_qkv(x, w, add, gain, shift, rows):
    total, d = x.shape
    width = w.shape[1] // 3
    whole = lambda a: pl.BlockSpec(a.shape, lambda i: (0, 0))
    return pl.pallas_call(
        ln_qkv_kernel,
        grid=(total // rows,),
        in_specs=[pl.BlockSpec((rows, d), lambda i: (i, 0)), whole(w), whole(add), whole(gain), whole(shift)],
        out_specs=[pl.BlockSpec((rows, d), lambda i: (i, 0))]
        + [pl.BlockSpec((rows, width), lambda i: (i, 0))] * 3,
        out_shape=[jax.ShapeDtypeStruct((total, d), BF)]
        + [jax.ShapeDtypeStruct((total, width), BF)] * 3,
        compiler_params=params(1),
        cost_estimate=cost(2 * total * d * 3 * width, total * d * 4 + total * width * 6),
        name="ln_qkv",
    )(x, w, add, gain, shift)


def ffn_kernel(n_ref, up_ref, we_ref, wr_ref, be_ref, out_ref, dn_ref, dwe_ref, dwr_ref, dbe_ref, nt):
    step = pl.program_id(0)

    @pl.when(step == 0)
    def _():
        nt[...] = n_ref[...].T
        out_ref[...] = jnp.zeros_like(out_ref)
        dn_ref[...] = jnp.zeros_like(dn_ref)

    we = we_ref[...]
    wr = wr_ref[...]
    up = up_ref[...]
    h = jnp.dot(n_ref[...], we, preferred_element_type=F32) + be_ref[...]
    half = 0.5 + 0.5 * lax.erf(h * (2.0**-0.5))
    act = (h * half).astype(BF)
    slope = half + h * jnp.exp(-0.5 * h * h) * ((2.0 * math.pi) ** -0.5)
    out_ref[...] += jnp.dot(act, wr, preferred_element_type=F32)
    da = lax.dot_general(up, wr, (((1,), (1,)), ((), ())), preferred_element_type=F32)
    dh32 = da * slope
    dh = dh32.astype(BF)
    dn_ref[...] += lax.dot_general(dh, we, (((1,), (1,)), ((), ())), preferred_element_type=F32)
    dwe_ref[...] = jnp.dot(nt[...], dh, preferred_element_type=F32).astype(BF)
    dwr_ref[...] = jnp.dot(act.T, up, preferred_element_type=F32).astype(BF)
    dbe_ref[...] = jnp.sum(dh.astype(F32), axis=0, keepdims=True)


def ffn(n, up, we, wr, be, chunk):
    rows, d = n.shape
    ff = we.shape[1]
    whole = pl.BlockSpec((rows, d), lambda i: (0, 0))
    return pl.pallas_call(
        ffn_kernel,
        grid=(ff // chunk,),
        in_specs=[
            whole,
            whole,
            pl.BlockSpec((d, chunk), lambda i: (0, i)),
            pl.BlockSpec((chunk, d), lambda i: (i, 0)),
            pl.BlockSpec((1, chunk), lambda i: (0, i)),
        ],
        out_specs=[
            whole,
            whole,
            pl.BlockSpec((d, chunk), lambda i: (0, i)),
            pl.BlockSpec((chunk, d), lambda i: (i, 0)),
            pl.BlockSpec((1, chunk), lambda i: (0, i)),
        ],
        out_shape=[
            jax.ShapeDtypeStruct((rows, d), F32),
            jax.ShapeDtypeStruct((rows, d), F32),
            jax.ShapeDtypeStruct((d, ff), BF),
            jax.ShapeDtypeStruct((ff, d), BF),
            jax.ShapeDtypeStruct((1, ff), F32),
        ],
        scratch_shapes=[pltpu.VMEM((d, rows), BF)],
        compiler_params=params(1),
        cost_estimate=cost(12 * rows * d * ff, 8 * d * ff + rows * d * 12, 2 * rows * ff),
        name="ffn",
    )(n, up, we, wr, be)


def layer_norm(input_rows, norm_gain, norm_shift):
    centre = jnp.mean(input_rows, axis=-1, keepdims=True)
    centered = input_rows - centre
    spread = jnp.mean(centered * centered, axis=-1, keepdims=True)
    return centered * lax.rsqrt(spread + EPS) * norm_gain + norm_shift


def mul(rows, matrix):
    return jnp.dot(rows, matrix, preferred_element_type=F32)


def mul_back(grad, matrix):
    return lax.dot_general(grad, matrix, (((1,), (1,)), ((), ())), preferred_element_type=F32)


def grad_of(rows, grad):
    return lax.dot_general(
        rows, grad, (((0,), (0,)), ((), ())), preferred_element_type=F32
    ).astype(BF)


def col_sum(grad):
    return jnp.sum(grad.astype(F32), axis=0)


def gather(x, axes):
    return lax.all_gather(x, axes, axis=0, tiled=True)


def scatter(x, axes):
    return lax.psum_scatter(x, axes, scatter_dimension=0, tiled=True)


CTX = ("g", "m")
ALL = ("g", "m", "fsdp")


def body(
    tokens, encoder_states, lengths, cotangent,
    first_gain, first_shift, query_weight, query_bias, key_weight, value_weight, value_bias,
    self_out_weight, self_out_bias, second_gain, second_shift,
    cross_query_weight, cross_query_bias, cross_key_weight, cross_value_weight, cross_value_bias,
    cross_out_weight, cross_out_bias, third_gain, third_shift,
    expand_weight, expand_bias, reduce_weight, reduce_bias,
):
    groups, members, fs = lax.axis_size("g"), lax.axis_size("m"), lax.axis_size("fsdp")
    gi, mi, fi = lax.axis_index("g"), lax.axis_index("m"), lax.axis_index("fsdp")
    ctx = groups * members
    me = gi * members + mi
    tokens, encoder, cotangent = tokens[0], encoder_states[0], cotangent[0]
    local, d = tokens.shape
    total = local * ctx
    shard = d // fs
    ff = expand_weight.shape[1]
    hg = HEADS // groups
    width = hg * HEAD_DIM
    piece = local // members
    frames = encoder.shape[0]
    kt = 512
    padded = -(-frames // kt) * kt
    length = lengths[0]

    vectors = [
        first_gain, first_shift, query_bias, value_bias, self_out_bias, second_gain, second_shift,
        cross_query_bias, cross_value_bias, cross_out_bias, third_gain, third_shift, reduce_bias,
    ]
    ratio = ff // d
    columns = jnp.concatenate(
        [jnp.stack(vectors, axis=1), expand_bias.reshape(shard, ratio)], axis=1
    )
    columns = jnp.pad(columns, ((0, 0), (0, 128 - columns.shape[1])))
    mine = lambda w: lax.dynamic_slice_in_dim(w, gi * width, width, 1)
    first = gather(
        jnp.concatenate([mine(query_weight), mine(key_weight), mine(value_weight), columns], axis=1),
        "fsdp",
    )
    all_tokens = gather(tokens, CTX)
    second = gather(
        jnp.concatenate(
            [self_out_weight, cross_query_weight, cross_key_weight, cross_value_weight, cross_out_weight],
            axis=1,
        ),
        "fsdp",
    )
    so_mat, cq_mat, ck_mat, cv_mat, co_mat = [second[:, i * d : (i + 1) * d] for i in range(5)]
    expand_mat = gather(expand_weight, "fsdp")
    reduce_mat = gather(reduce_weight, "fsdp")
    by_group = lambda w: w.reshape(shard, groups, width)
    qkv_mat = gather(
        jnp.stack([by_group(query_weight), by_group(key_weight), by_group(value_weight)], axis=2).reshape(
            shard, 3 * d
        ),
        "fsdp",
    )
    table = first[:, 3 * width :].astype(F32).T
    (
        gain_one, shift_one, query_add, value_add, so_add, gain_two, shift_two,
        cq_add, cv_add, co_add, gain_three, shift_three, reduce_add,
    ) = [table[i] for i in range(len(vectors))]
    expand_add = first[:, 3 * width + len(vectors) : 3 * width + len(vectors) + ratio].astype(F32).reshape(1, ff)

    own_part = lambda v: lax.dynamic_slice_in_dim(v, gi * width, width, 0)
    qkv_add = jnp.concatenate([own_part(query_add), jnp.zeros((width,), F32), own_part(value_add)])
    normed_all, q, k, v = ln_qkv(
        all_tokens, first[:, : 3 * width], qkv_add[None], gain_one[None], shift_one[None], min(512, total)
    )
    info = jnp.stack([length, mi.astype(jnp.int32)])
    q_index = lambda i, s: i * members + (s[1] + i) % members
    rows_of = lambda i, s: q_index(i, s) * piece
    mixed32, mixed_own, lse = flash_fwd(
        q, k, v, info, hg, piece, kt, True, ctx, q_index, rows_of, "self_fwd"
    )

    def exchange(x):
        return lax.all_to_all(x, CTX, 0, 0, tiled=True)

    def to_rows(x, cols):
        x = x.reshape(groups, members, piece, cols)
        x = lax.dynamic_slice_in_dim(jnp.concatenate([x, x], axis=1), (-me) % members, members, 1)
        return x.transpose(1, 2, 0, 3).reshape(local, groups * cols)

    def to_heads(x):
        x = x.reshape(members, piece, groups, width)
        x = lax.dynamic_slice_in_dim(jnp.concatenate([x, x], axis=0), me % members, members, 0)
        return x.transpose(2, 0, 1, 3).reshape(ctx * piece, width)

    mixed = to_rows(exchange(mixed_own), width)

    residual = tokens.astype(F32)
    after_self = residual + mul(mixed, so_mat) + so_add
    normed_two, norm_back_two = jax.vjp(layer_norm, after_self, gain_two, shift_two)
    normed_two = normed_two.astype(BF)
    cross_query = (mul(normed_two, cq_mat) + cq_add).astype(BF)
    enc = jnp.pad(encoder, ((0, padded - frames), (0, 0)))
    cross_keys = mul(enc, ck_mat).astype(BF)
    cross_values = (mul(enc, cv_mat) + cv_add).astype(BF)
    cross_info = jnp.array([frames, 0], jnp.int32)
    cqt = min(256, local)
    plain = lambda i, s: i
    zero = lambda i, s: 0
    chg = 4
    cross32, cross_rows, cross_lse = flash_fwd(
        cross_query, cross_keys, cross_values, cross_info, chg, cqt, kt, False, local // cqt, plain, zero,
        "cross_fwd",
    )
    after_cross = after_self + mul(cross_rows, co_mat) + co_add
    normed_three, norm_back_three = jax.vjp(layer_norm, after_cross, gain_three, shift_three)
    normed_three = normed_three.astype(BF)

    position = me * local + jnp.arange(local, dtype=jnp.int32)
    valid = (position < length).astype(F32)[:, None]
    up = cotangent.astype(F32) * valid
    reduce_up = up.astype(BF)
    ff_out, ff_back, grad_expand, grad_reduce, grad_expand_add = ffn(
        normed_three, reduce_up, expand_mat, reduce_mat, expand_add, 512
    )
    layer_out = (after_cross + ff_out + reduce_add) * valid
    expand_shard = lax.psum(scatter(grad_expand, "fsdp"), CTX)
    reduce_shard = lax.psum(scatter(grad_reduce, "fsdp"), CTX)
    part, grad_gain_three, grad_shift_three = norm_back_three(ff_back)
    up = up + part

    co_up = up.astype(BF)
    cross_dout = mul_back(co_up, co_mat).astype(BF)
    cq_up, ck_part, cv_part = flash_bwd(
        cross_query, cross_dout, cross32, cross_lse, cross_keys, cross_values, cross_info, chg, cqt, kt,
        False, local // cqt, plain, zero, "cross_bwd",
    )
    enc_up = scatter(jnp.concatenate([ck_part, cv_part], axis=1), CTX)
    enc_rows_count = padded // ctx
    enc_rows = lax.dynamic_slice_in_dim(enc, me * enc_rows_count, enc_rows_count, 0)
    enc_grad_rows = mul_back(enc_up[:, :d], ck_mat) + mul_back(enc_up[:, d:], cv_mat)
    encoder_grads = gather(enc_grad_rows.astype(BF), CTX)[:frames].astype(F32)
    grad_ckv = grad_of(enc_rows, enc_up)
    part, grad_gain_two, grad_shift_two = norm_back_two(mul_back(cq_up, cq_mat))
    up = up + part
    so_up = up.astype(BF)

    self_dout = mul_back(so_up, so_mat).astype(BF)
    dout_own = exchange(to_heads(self_dout))
    grad_mid = jnp.concatenate(
        [grad_of(mixed, so_up), grad_of(normed_two, cq_up), grad_of(cross_rows, co_up)], axis=1
    )
    q_up, k_part, v_part = flash_bwd(
        q, dout_own, mixed32, lse, k, v, info, hg, piece, kt, True, ctx, q_index, rows_of, "self_bwd"
    )
    mid_shard = lax.psum(scatter(grad_mid, "fsdp"), CTX)
    ckv_shard = lax.psum(scatter(grad_ckv, "fsdp"), CTX)

    def pick(x, member):
        x = x.reshape(ctx, members, piece, x.shape[-1])
        which = ((member + jnp.arange(ctx)) % members)[:, None, None]
        out = x[:, 0]
        for c in range(1, members):
            out = jnp.where(which == c, x[:, c], out)
        return out.reshape(ctx * piece, x.shape[-1])

    kv_part = jnp.concatenate([k_part, v_part], axis=1)
    kv_up = pick(kv_part, mi).astype(F32)
    for hop in range(1, members):
        kv_up = kv_up + lax.ppermute(
            pick(kv_part, mi + hop), "m", [(i, (i + hop) % members) for i in range(members)]
        ).astype(F32)
    qkv_up = jnp.concatenate([q_up, kv_up.astype(BF)], axis=1)
    qkv_rows = to_rows(exchange(qkv_up), 3 * width)
    grad_qkv = grad_of(pick(normed_all, mi), qkv_up)
    qkv_shard = gather(lax.psum(scatter(grad_qkv, "fsdp"), "m"), "g").reshape(groups, shard, 3, width)
    query_shard, key_shard, value_shard = [
        qkv_shard[:, :, i].transpose(1, 0, 2).reshape(shard, d) for i in range(3)
    ]
    _, norm_back_one = jax.vjp(layer_norm, residual, gain_one, shift_one)
    part, grad_gain_one, grad_shift_one = norm_back_one(mul_back(qkv_rows, qkv_mat))
    token_grads = up + part

    def place(x):
        return lax.dynamic_update_slice_in_dim(jnp.zeros((d,), F32), x, gi * width, 0)

    sums = jnp.stack(
        [
            grad_gain_one, grad_shift_one,
            place(col_sum(q_up)), place(col_sum(qkv_up[:, 2 * width :])),
            col_sum(so_up), grad_gain_two, grad_shift_two,
            col_sum(cq_up), col_sum(enc_up[:, d:]), col_sum(co_up),
            grad_gain_three, grad_shift_three, col_sum(reduce_up),
        ]
    )
    sums = jnp.concatenate([sums, grad_expand_add.reshape(ratio, d)], axis=0)
    sums = lax.psum(sums, ALL)
    vec = lax.dynamic_slice_in_dim(sums[: len(vectors)], fi * shard, shard, 1)
    expand_vec = lax.dynamic_slice_in_dim(sums[len(vectors) :].reshape(ff), fi * (ff // fs), ff // fs, 0)
    vec = [vec[i] for i in range(len(vectors))]
    f32 = lambda x: x.astype(F32)
    mid = [f32(mid_shard[:, i * d : (i + 1) * d]) for i in range(3)]
    return (
        layer_out[None], token_grads[None], encoder_grads[None],
        vec[0], vec[1], f32(query_shard), vec[2], f32(key_shard), f32(value_shard), vec[3],
        mid[0], vec[4], vec[5], vec[6], mid[1], vec[7],
        f32(ckv_shard[:, :d]), f32(ckv_shard[:, d:]), vec[8], mid[2], vec[9],
        vec[10], vec[11], f32(expand_shard), expand_vec, f32(reduce_shard), vec[12],
    )


def solution(mesh):
    ctx, fs = mesh.shape["ctx"], mesh.shape["fsdp"]
    groups = math.gcd(HEADS, ctx // 2)
    split = Mesh(mesh.devices.reshape(groups, ctx // groups, fs), ("g", "m", "fsdp"))
    rows, slot, vec, mat = P("fsdp", CTX, None), P("fsdp", None, None), P("fsdp"), P("fsdp", None)
    weights = (
        vec, vec, mat, vec, mat, mat, vec, mat, vec, vec, vec, mat, vec, mat, mat, vec, mat, vec,
        vec, vec, mat, vec, mat, vec,
    )
    return jax.shard_map(
        body,
        mesh=split,
        in_specs=(rows, slot, vec, rows) + weights,
        out_specs=(rows, rows, slot) + weights,
        check_vma=False,
    )
```

time: 1710 us -> 1020 us (0.60)
  matrix products: 517 us -> 50.6 us
  waiting for transfers between devices: 777 us -> 523 us
  Pallas kernels: 0 us -> 158 us
  other arithmetic: 173 us -> 49.9 us
  local copies, waits for them, and re-layouts: 152 us -> 103 us
  blocking collectives: 58.3 us -> 98.1 us
    dot_general x91 -> x16, matrix products: 496 us -> 50.6 us  [the longest x6 18.7 us: mul_back(): lax.dot_general(grad, matrix, (((1,), (1,)), ((), ())), preferred_element...]
    pallas_call x0 -> x6, Pallas kernels: none -> 158 us  [the longest x2 79.1 us: flash_bwd(): pl.pallas_call(functools.partial(bwd_kernel, hg, qt, kt, causal, rows_of)...]
    reduce_scatter x10 -> x5, waiting for transfers between devices: 384 us -> 237 us  [scatter(): return lax.psum_scatter(x, axes, scatter_dimension=0, tiled=True)]
    psum x1 -> x2, waiting for transfers between devices: 187 us -> 57.3 us  [the longest x1 57.3 us: body(): mid_shard = lax.psum(scatter(grad_mid, 'fsdp'), CTX)]
    reduce_sum x18 -> x9, other arithmetic: 75.1 us -> 7.9 us  [the longest x7 4.36 us: col_sum(): return jnp.sum(grad.astype(F32), axis=0)]
    all_gather x1, blocking collectives: 8.29 us -> 56.6 us  [gather(): return lax.all_gather(x, axes, axis=0, tiled=True)]
    convert_element_type x39 -> x8, other arithmetic: 50.5 us -> 11.1 us  [the longest x5 6.97 us: body(): f32 = lambda x: x.astype(F32)]
    dynamic_slice x32 -> x5, local copies, waits for them, and re-layouts: 43.2 us -> 3.79 us  [the longest x3 3.04 us: body(): mine = lambda w: lax.dynamic_slice_in_dim(w, gi * width, width, 1)]
  transfers between devices with their start and end apart: 25 -> 19, of which waited for: 17 -> 13; matrix products, arithmetic and copies ran while one was open for 26% -> 13% of each run, Pallas kernels for 0% -> 6%
where the time goes in v1:
time: 1020 us; the launch traced here: 1010 us
  waiting for transfers between devices  523 us (51%)
  Pallas kernels  158 us (15%)
  local copies, waits for them, and re-layouts  103 us (10%)
  blocking collectives  98.1 us (10%)
  matrix products  50.6 us (5%)
  other arithmetic  49.9 us (5%)
  between operations  15.9 us (2%)
  starting transfers between devices  13.6 us (1%)
    reduce_scatter x5, waiting for transfers between devices, scatter(): return lax.psum_scatter(x, axes, scatter_dimension=0, tiled=True)  237 us
    all_gather x7, waiting for transfers between devices, gather(): return lax.all_gather(x, axes, axis=0, tiled=True)  204 us
    pallas_call x2, Pallas kernels, flash_bwd(): pl.pallas_call(functools.partial(bwd_kernel, hg, qt, kt, causal, rows_of)...  79.1 us
    psum x1, waiting for transfers between devices, body(): mid_shard = lax.psum(scatter(grad_mid, 'fsdp'), CTX)  57.3 us
    all_gather x1, blocking collectives, gather(): return lax.all_gather(x, axes, axis=0, tiled=True)  56.6 us
    unnamed x131, local copies, waits for them, and re-layouts  45.3 us
    pallas_call x2, Pallas kernels, flash_fwd(): pl.pallas_call(functools.partial(fwd_kernel, hg, qt, kt, causal, rows_of)...  45 us
    psum x1, blocking collectives, body(): sums = lax.psum(sums, ALL)  41.5 us
  transfers between devices with their start and end apart: 19, of which 13 were waited for; matrix products, arithmetic and copies ran while one was open for 13% of the time, Pallas kernels for 6%

profile of v1, /device:TPU:0, one launch (start us, length us, event | category | flops | bytes accessed | tf_op | source)
XLA Modules:
  0.0 1012.5 jit_solution(8381800458101287897)
XLA Ops:
  26.8 25.8 %all-gather.9.cloned.1.call-done = bf16[768,704]{1,0:T(8,128)(2,1)} async-done(((bf16[192,704]{1,0:T(8,128)(2,1)}), bf16[768,704]{1,0:T(8,128)(2,1)}) %all-gather.9.cloned.1.call-update) | async-done | bytes 1081360 | tf_op jit(solution)/shard_map/all_gather | solution.py:411
  57.0 62.0 %all-gather.21.cloned.1.call-done = bf16[1,4096,768]{2,1,0:T(8,128)(2,1)} async-done(((bf16[1,512,768]{2,1,0:T(8,128)(2,1)}), bf16[1,4096,768]{2,1,0:T(8,128)(2,1)}) %all-gather.21.cloned.1.call-update) | async-done | bytes 6291472 | tf_op jit(solution)/shard_map/all_gather | solution.py:411
  119.0 13.6 %ln_qkv.1 = (bf16[4096,768]{1,0:T(8,128)(2,1)}, bf16[4096,192]{1,0:T(8,128)(2,1)}, bf16[4096,192]{1,0:T(8,128)(2,1)}, bf16[4096,192]{1,0:T(8,128)(2,1)}) custom-call(bf16[4096,768]{1,0:T(8,128)(2,1)} %bitcast.184, bf16[768,576]{1,0:T(8,128)(2,1)} %slice.211.w_ref, f32[1,576]{1,0:T(1,128)} %broadcast_in_dim.76.add_ref, f32[1,768]{1,0:T(1,128)} %get-tuple-element.334.gain_ref, ...), custom_call_target="tpu_custom_call" | custom-call | flops 3623878656 | bytes 17301504 | tf_op jit(solution)/shard_map/ln_qkv/pallas_call | solution.py:310
  132.6 24.2 %self_fwd.1 = (f32[2048,192]{1,0:T(8,128)}, bf16[2048,192]{1,0:T(8,128)(2,1)}, f32[1,8,3,256]{3,2,1,0:T(4,128)}) custom-call(s32[2]{0:T(128)} %pad_add_fusion.info, bf16[4096,192]{1,0:T(8,128)(2,1)} %get-tuple-element.48.q_ref, bf16[4096,192]{1,0:T(8,128)(2,1)} %get-tuple-element.49.k_ref, bf16[4096,192]{1,0:T(8,128)(2,1)} %get-tuple-element.50.v_ref), custom_call_target="tpu_custom_call" | custom-call | flops 12884901888 | bytes 6291456 | tf_op jit(solution)/shard_map/self_fwd/pallas_call | solution.py:210
  165.6 21.3 %all-gather.11.cloned.1.call-done = bf16[768,3840]{1,0:T(8,128)(2,1)} async-done(((bf16[192,3840]{1,0:T(8,128)(2,1)}), bf16[768,3840]{1,0:T(8,128)(2,1)}) %all-gather.11.cloned.1.call-update) | async-done | bytes 5898256 | tf_op jit(solution)/shard_map/all_gather | solution.py:411
  186.8 5.5 convolution_convert_fusion.1.k_ref
  204.5 20.7 %cross_fwd.1 = (f32[512,768]{1,0:T(8,128)}, bf16[512,768]{1,0:T(8,128)(2,1)}, f32[3,2,4,256]{3,2,1,0:T(4,128)}) custom-call(s32[2]{0:T(128)} %constant.92.clone.info, bf16[512,768]{1,0:T(8,128)(2,1)} %add_convert_fusion.3.q_ref, bf16[1536,768]{1,0:T(8,128)(2,1)} %convolution_convert_fusion.1.k_ref, bf16[1536,768]{1,0:T(8,128)(2,1)} %add_convert_fusion.v_ref), custom_call_target="tpu_custom_call" | custom-call | flops 9663676416 | bytes 7864320 | tf_op jit(solution)/shard_map/cross_fwd/pallas_call | solution.py:210
  229.2 16.4 %all-gather.13.cloned.1.call-done.we_ref = bf16[768,3072]{1,0:T(8,128)(2,1)} async-done(((bf16[192,3072]{1,0:T(8,128)(2,1)}), bf16[768,3072]{1,0:T(8,128)(2,1)}) %all-gather.13.cloned.1.call-update) | async-done | bytes 4718608 | tf_op jit(solution)/shard_map/all_gather | solution.py:411
  245.5 58.7 %all-gather.15.cloned.1.call-done.wr_ref = bf16[3072,768]{1,0:T(8,128)(2,1)} async-done(((bf16[768,768]{1,0:T(8,128)(2,1)}), bf16[3072,768]{1,0:T(8,128)(2,1)}) %all-gather.15.cloned.1.call-update) | async-done | bytes 4718608 | tf_op jit(solution)/shard_map/all_gather | solution.py:411
  304.2 20.8 %ffn.1 = (f32[512,768]{1,0:T(8,128)}, f32[512,768]{1,0:T(8,128)}, bf16[768,3072]{1,0:T(8,128)(2,1)}, bf16[3072,768]{1,0:T(8,128)(2,1)}, f32[1,3072]{1,0:T(1,128)}) custom-call(bf16[512,768]{1,0:T(8,128)(2,1)} %add_convert_fusion.2.n_ref, bf16[512,768]{1,0:T(8,128)(2,1)} %get-tuple-element.311.up_ref, bf16[768,3072]{1,0:T(8,128)(2,1)} %all-gather.13.cloned.1.call-done.we_ref, ...), custom_call_target="tpu_custom_call" | custom-call | flops 14495514624 | bytes 23592960 | tf_op jit(solution)/shard_map/ffn/pallas_call | solution.py:354
  333.4 37.7 %cross_bwd.1 = (bf16[512,768]{1,0:T(8,128)(2,1)}, bf16[1536,768]{1,0:T(8,128)(2,1)}, bf16[1536,768]{1,0:T(8,128)(2,1)}) custom-call(s32[2]{0:T(128)} %constant.92.clone.info, bf16[512,768]{1,0:T(8,128)(2,1)} %add_convert_fusion.3.q_ref, bf16[512,768]{1,0:T(8,128)(2,1)} %convolution_convert_fusion.7.do_ref, f32[512,768]{1,0:T(8,128)} %get-tuple-element.55.o_ref, ...), custom_call_target="tpu_custom_call" | custom-call | flops 24159191040 | bytes 13369344 | tf_op jit(solution)/shard_map/cross_bwd/pallas_call | solution.py:250
  387.7 20.8 %all-to-all-done.1 = bf16[8,256,192]{1,2,0:T(8,128)(2,1)S(1)} async-done(((bf16[8,256,192]{1,2,0:T(8,128)(2,1)}), bf16[8,256,192]{1,2,0:T(8,128)(2,1)S(1)}, u32[]{:S(2)}, u32[]{:S(2)}) %all-to-all-start.1) | async-done | bytes 786464 | tf_op jit(solution)/shard_map/all_to_all | solution.py:499
  409.9 41.4 %self_bwd.1 = (bf16[2048,192]{1,0:T(8,128)(2,1)}, bf16[4096,192]{1,0:T(8,128)(2,1)}, bf16[4096,192]{1,0:T(8,128)(2,1)}) custom-call(s32[2]{0:T(128)} %pad_add_fusion.info, bf16[4096,192]{1,0:T(8,128)(2,1)} %get-tuple-element.48.q_ref, bf16[2048,192]{1,0:T(8,128)(2,1)} %bitcast.165, f32[2048,192]{1,0:T(8,128)} %get-tuple-element.58.o_ref, ...), custom_call_target="tpu_custom_call" | custom-call | flops 32212254720 | bytes 10223616 | tf_op jit(solution)/shard_map/self_bwd/pallas_call | solution.py:250
  492.2 35.0 %reduce-scatter.11.cloned.1.call-done = bf16[192,576]{1,0:T(8,128)(2,1)} async-done(((bf16[768,576]{1,0:T(8,128)(2,1)}), bf16[192,576]{1,0:T(8,128)(2,1)}) %reduce-scatter.11.cloned.1.call-update) | async-done | bytes 221200 | tf_op jit(solution)/shard_map/reduce_scatter | solution.py:415
  537.9 46.6 %reduce-scatter.9.cloned.1.call-done = bf16[192,1536]{1,0:T(8,128)(2,1)} async-done(((bf16[1536,1536]{1,0:T(8,128)(2,1)}), bf16[192,1536]{1,0:T(8,128)(2,1)}) %reduce-scatter.9.cloned.1.call-update) | async-done | bytes 589840 | tf_op jit(solution)/shard_map/reduce_scatter | solution.py:415
  609.1 56.6 %all_gather.31 = bf16[768,576]{1,0:T(8,128)(2,1)S(1)} all-gather(bf16[192,576]{1,0:T(8,128)(2,1)} %all-reduce.6.cloned.1.call-done), channel_id=1, replica_groups=mesh['g'=4,'m'=2,'fsdp'=4] {'g'}, dimensions={0}, use_global_device_ids=true | all-gather | bytes 1105920 | tf_op jit(solution)/shard_map/all_gather | solution.py:411
  684.0 20.4 %all-gather.17.cloned.1.call-done = bf16[768,2304]{1,0:T(8,128)(2,1)} async-done(((bf16[192,2304]{1,0:T(8,128)(2,1)}), bf16[768,2304]{1,0:T(8,128)(2,1)}) %all-gather.17.cloned.1.call-update) | async-done | bytes 3538960 | tf_op jit(solution)/shard_map/all_gather | solution.py:411
  704.4 5.1 fusion.55
  709.5 54.9 %reduce-scatter.15.cloned.1.call-done = bf16[192,3072]{1,0:T(8,128)(2,1)} async-done(((bf16[768,3072]{1,0:T(8,128)(2,1)}), bf16[192,3072]{1,0:T(8,128)(2,1)}) %reduce-scatter.15.cloned.1.call-update) | async-done | bytes 1179664 | tf_op jit(solution)/shard_map/reduce_scatter | solution.py:415
  764.4 59.8 %reduce-scatter.17.cloned.1.call-done = bf16[768,768]{1,0:T(8,128)(2,1)} async-done(((bf16[3072,768]{1,0:T(8,128)(2,1)}), bf16[768,768]{1,0:T(8,128)(2,1)}) %reduce-scatter.17.cloned.1.call-update) | async-done | bytes 1179664 | tf_op jit(solution)/shard_map/reduce_scatter | solution.py:415
  824.2 41.0 %reduce-scatter.13.cloned.1.call-done = bf16[192,1536]{1,0:T(8,128)(2,1)} async-done(((bf16[768,1536]{1,0:T(8,128)(2,1)}), bf16[192,1536]{1,0:T(8,128)(2,1)}) %reduce-scatter.13.cloned.1.call-update) | async-done | bytes 589840 | tf_op jit(solution)/shard_map/reduce_scatter | solution.py:415
  868.8 41.5 %psum.42 = f32[17,768]{1,0:T(8,128)S(1)} all-reduce(f32[17,768]{1,0:T(8,128)S(1)} %concatenate.46), channel_id=1, replica_groups=mesh['g'=4,'m'=2,'fsdp'=4] {'g','m','fsdp'}, use_global_device_ids=true, to_apply=%region_26.27 | all-reduce | flops 13056 | bytes 104448 | tf_op jit(solution)/shard_map/psum | solution.py:612
  913.8 25.8 %copy.250 = f32[1,1500,768]{2,0,1:T(1,128)} copy(f32[1,1500,768]{2,1,0:T(8,128)S(1)} %fusion.2) | data formatting | bytes 9216000
  939.6 57.3 %all-reduce.8.cloned.1.call-done = (bf16[192,2304]{0,1:T(8,128)(2,1)}, bf16[192,1536]{1,0:T(8,128)(2,1)}, bf16[192,3072]{1,0:T(8,128)(2,1)}, bf16[768,768]{1,0:T(8,128)(2,1)}) async-done(((bf16[192,2304]{0,1:T(8,128)(2,1)}, bf16[192,1536]{1,0:T(8,128)(2,1)}, bf16[192,3072]{1,0:T(8,128)(2,1)}, bf16[768,768]{1,0:T(8,128)(2,1)}), (bf16[192,2304]{0,1:T(8,128)(2,1)}, bf16[192,1536]{1,0:T(8,128)(2,1)}, ...) | async-done | bytes 3833872 | tf_op jit(solution)/shard_map/psum | solution.py:571
  (314 shorter events, 183.8 us)
Async XLA Ops:
  7.2 45.4 %all-gather.9.cloned.1.call-start = ((), (), s32[]{:S(2)}) async-start(), calls=%async_computation.9 | async-start | bytes 1474560 | tf_op jit(solution)/shard_map/all_gather | solution.py:411
  22.2 96.8 %all-gather.21.cloned.1.call-start = ((), (), s32[]{:S(2)}) async-start(), calls=%async_computation.21 | async-start | bytes 7077888 | tf_op jit(solution)/shard_map/all_gather | solution.py:411
  22.9 163.9 %all-gather.11.cloned.1.call-start = ((), (), s32[]{:S(2)}) async-start(), calls=%async_computation.10 | async-start | bytes 7372800 | tf_op jit(solution)/shard_map/all_gather | solution.py:411
  24.4 221.1 %all-gather.13.cloned.1.call-start = ((), (), s32[]{:S(2)}) async-start(), calls=%async_computation.11 | async-start | bytes 5898240 | tf_op jit(solution)/shard_map/all_gather | solution.py:411
  25.0 279.2 %all-gather.15.cloned.1.call-start = ((), (), s32[]{:S(2)}) async-start(), calls=%async_computation.12 | async-start | bytes 5898240 | tf_op jit(solution)/shard_map/all_gather | solution.py:411
  159.1 38.0 %all-to-all-start = ((bf16[8,256,192]{1,2,0:T(8,128)(2,1)}), bf16[8,256,192]{1,2,0:T(8,128)(2,1)S(1)}, u32[]{:S(2)}, u32[]{:S(2)}) async-start(bf16[8,256,192]{1,2,0:T(8,128)(2,1)} %copy.232), calls=%async_computation | async-start | bytes 1572864 | tf_op jit(solution)/shard_map/all_to_all | solution.py:499
  200.9 24.4 %copy-start.9 = (f32[512,768]{1,0:T(8,128)}, f32[512,768]{1,0:T(8,128)S(1)}, u32[]{:S(2)}) copy-start(f32[512,768]{1,0:T(8,128)S(1)} %get-tuple-element.353) | copy-start | bytes 4718596
  333.4 37.7 %copy-start.10 = (f32[512,768]{1,0:T(8,128)S(1)}, f32[512,768]{1,0:T(8,128)}, u32[]{:S(2)}) copy-start(f32[512,768]{1,0:T(8,128)} %copy-done.9) | copy-start | bytes 4718596
  375.9 112.4 %copy-start = (f32[512,768]{1,0:T(8,128)}, f32[512,768]{1,0:T(8,128)S(1)}, u32[]{:S(2)}) copy-start(f32[512,768]{1,0:T(8,128)S(1)} %get-tuple-element.315) | copy-start | bytes 4718596
  382.9 25.5 %all-to-all-start.1 = ((bf16[8,256,192]{1,2,0:T(8,128)(2,1)}), bf16[8,256,192]{1,2,0:T(8,128)(2,1)S(1)}, u32[]{:S(2)}, u32[]{:S(2)}) async-start(bf16[8,256,192]{1,2,0:T(8,128)(2,1)} %bitcast.14), calls=%async_computation.1 | async-start | bytes 1572864 | tf_op jit(solution)/shard_map/all_to_all | solution.py:499
  387.5 139.8 %reduce-scatter.11.cloned.1.call-start = ((), (), s32[]{:S(2)}) async-start(), calls=%async_computation.16 | async-start | bytes 1228800 | tf_op jit(solution)/shard_map/reduce_scatter | solution.py:415
  463.8 7.9 collective-permute-start
  479.3 105.1 %reduce-scatter.9.cloned.1.call-start = ((), (), s32[]{:S(2)}) async-start(), calls=%async_computation.14 | async-start | bytes 5308416 | tf_op jit(solution)/shard_map/reduce_scatter | solution.py:415
  484.3 124.8 %all-reduce.6.cloned.1.call-start = ((), (), s32[]{:S(2)}) async-start(), calls=%async_computation.17 | async-start | bytes 491520 | tf_op jit(solution)/shard_map/psum | solution.py:591
  527.3 154.2 %reduce-scatter.19.cloned.1.call-start = ((), (), s32[]{:S(2)}) async-start(), calls=%async_computation.22 | async-start | bytes 4423680
  533.4 171.0 %all-gather.17.cloned.1.call-start = ((), (), s32[]{:S(2)}) async-start(), calls=%async_computation.13 | async-start | bytes 4423680 | tf_op jit(solution)/shard_map/all_gather | solution.py:411
  536.5 227.9 %reduce-scatter.15.cloned.1.call-start = ((), (), s32[]{:S(2)}) async-start(), calls=%async_computation.19 | async-start | bytes 5898240 | tf_op jit(solution)/shard_map/reduce_scatter | solution.py:415
  537.2 287.0 %reduce-scatter.17.cloned.1.call-start = ((), (), s32[]{:S(2)}) async-start(), calls=%async_computation.20 | async-start | bytes 5898240 | tf_op jit(solution)/shard_map/reduce_scatter | solution.py:415
  537.3 47.2 %copy-start.20 = (bf16[1,1500,768]{2,1,0:T(8,128)(2,1)S(1)}, bf16[1,1500,768]{2,1,0:T(8,128)(2,1)}, u32[]{:S(2)}) copy-start(bf16[1,1500,768]{2,1,0:T(8,128)(2,1)} %param.30) | copy-start | bytes 6912004
  537.8 327.4 %reduce-scatter.13.cloned.1.call-start = ((), (), s32[]{:S(2)}) async-start(), calls=%async_computation.18 | async-start | bytes 2949120 | tf_op jit(solution)/shard_map/reduce_scatter | solution.py:415
  591.1 83.6 %all-to-all-start.2 = ((bf16[8,256,576]{1,2,0:T(8,128)(2,1)}), bf16[8,256,576]{1,2,0:T(8,128)(2,1)}, u32[]{:S(2)}, u32[]{:S(2)}) async-start(bf16[8,256,576]{1,2,0:T(8,128)(2,1)} %bitcast.147), calls=%async_computation.2 | async-start | bytes 4718592 | tf_op jit(solution)/shard_map/all_to_all | solution.py:499
  595.6 316.1 %all-gather.19.cloned.1.call-start = ((), (), s32[]{:S(2)}) async-start(), calls=%async_computation.15 | async-start | bytes 2654208 | tf_op jit(solution)/shard_map/all_gather | solution.py:411
  600.2 396.6 %all-reduce.8.cloned.1.call-start = ((), (), s32[]{:S(2)}) async-start(), calls=%async_computation.23 | async-start | bytes 8257536 | tf_op jit(solution)/shard_map/psum | solution.py:571
  681.5 22.9 %copy-start.40 = (f32[768]{0:T(1024)S(1)}, f32[768]{0:T(1024)}, u32[]{:S(2)}) copy-start(f32[768]{0:T(1024)} %get-tuple-element.296) | copy-start | bytes 9220
  (54 other events, 151.2 us)
Sparse Core Ops, SparseCore 0:
  22.3 30.2 all-gather.8
  54.2 64.6 all-gather.20
  121.4 65.3 all-gather.10
  188.5 56.9 all-gather.12
  247.2 56.9 all-gather.14
  479.5 47.7 reduce-scatter.10
  529.6 54.8 reduce-scatter.8
  586.8 16.5 all-reduce.5
  607.1 48.3 reduce-scatter.18
  657.2 47.1 all-gather.16
  707.4 56.9 reduce-scatter.14
  767.2 56.9 reduce-scatter.16
  827.8 37.3 reduce-scatter.12
  867.3 32.1 all-gather.18
  902.0 94.8 all-reduce.7

commit v2 on v1

--- a/solution.py
+++ b/solution.py
@@ -415,8 +415,10 @@
     return lax.psum_scatter(x, axes, scatter_dimension=0, tiled=True)
 
 
-CTX = ("g", "m")
-ALL = ("g", "m", "fsdp")
+CHIPS = ("g", "p")
+CTX = ("g", "p", "c")
+ALL = ("g", "p", "c", "fsdp")
+SWAP = [(0, 1), (1, 0)]
 
 
 def body(
@@ -427,8 +429,10 @@
     cross_out_weight, cross_out_bias, third_gain, third_shift,
     expand_weight, expand_bias, reduce_weight, reduce_bias,
 ):
-    groups, members, fs = lax.axis_size("g"), lax.axis_size("m"), lax.axis_size("fsdp")
-    gi, mi, fi = lax.axis_index("g"), lax.axis_index("m"), lax.axis_index("fsdp")
+    groups, fs = lax.axis_size("g"), lax.axis_size("fsdp")
+    members = lax.axis_size(("p", "c"))
+    gi, mi, fi = lax.axis_index("g"), lax.axis_index(("p", "c")), lax.axis_index("fsdp")
+    core = lax.axis_index("c")
     ctx = groups * members
     me = gi * members + mi
     tokens, encoder, cotangent = tokens[0], encoder_states[0], cotangent[0]
@@ -509,6 +513,22 @@
         return x.transpose(2, 0, 1, 3).reshape(ctx * piece, width)
 
     mixed = to_rows(exchange(mixed_own), width)
+
+    def half(x, which):
+        return lax.dynamic_slice_in_dim(x, which * (x.shape[1] // 2), x.shape[1] // 2, 1)
+
+    def on_chip(x):
+        other = lax.ppermute(half(x, 1 - core), "c", SWAP)
+        return (half(x, core).astype(F32) + other.astype(F32)).astype(BF)
+
+    def over_fsdp(x):
+        x = lax.all_to_all(x.reshape(fs, x.shape[0] // fs, x.shape[1]), "fsdp", 0, 0)
+        return jnp.sum(x.astype(F32), axis=0).astype(BF)
+
+    def whole(x):
+        other = lax.ppermute(x, "c", SWAP)
+        low, high = jnp.where(core == 0, x, other), jnp.where(core == 0, other, x)
+        return jnp.concatenate([low, high], axis=1).astype(F32)
 
     residual = tokens.astype(F32)
     after_self = residual + mul(mixed, so_mat) + so_add
@@ -539,37 +559,46 @@
         normed_three, reduce_up, expand_mat, reduce_mat, expand_add, 512
     )
     layer_out = (after_cross + ff_out + reduce_add) * valid
-    expand_shard = lax.psum(scatter(grad_expand, "fsdp"), CTX)
-    reduce_shard = lax.psum(scatter(grad_reduce, "fsdp"), CTX)
+    ffn_shards = [over_fsdp(on_chip(grad_expand)), over_fsdp(on_chip(grad_reduce))]
     part, grad_gain_three, grad_shift_three = norm_back_three(ff_back)
     up = up + part
 
     co_up = up.astype(BF)
     cross_dout = mul_back(co_up, co_mat).astype(BF)
+    cross_dout, qkv_mat = lax.optimization_barrier((cross_dout, qkv_mat))
     cq_up, ck_part, cv_part = flash_bwd(
         cross_query, cross_dout, cross32, cross_lse, cross_keys, cross_values, cross_info, chg, cqt, kt,
         False, local // cqt, plain, zero, "cross_bwd",
     )
+    cq_up, ffn_shards = lax.optimization_barrier((cq_up, ffn_shards))
     enc_up = scatter(jnp.concatenate([ck_part, cv_part], axis=1), CTX)
     enc_rows_count = padded // ctx
     enc_rows = lax.dynamic_slice_in_dim(enc, me * enc_rows_count, enc_rows_count, 0)
+    part, grad_gain_two, grad_shift_two = norm_back_two(mul_back(cq_up, cq_mat))
+    up = up + part
+    so_up = up.astype(BF)
+
+    self_dout = mul_back(so_up, so_mat).astype(BF)
+    grad_mid = on_chip(
+        jnp.concatenate(
+        [grad_of(mixed, so_up), grad_of(normed_two, cq_up), grad_of(cross_rows, co_up)], axis=1
+        )
+    )
+    dout_own = exchange(to_heads(self_dout))
+    dout_own, grad_mid = lax.optimization_barrier((dout_own, grad_mid))
+    q_up, k_part, v_part = flash_bwd(
+        q, dout_own, mixed32, lse, k, v, info, hg, piece, kt, True, ctx, q_index, rows_of, "self_bwd"
+    )
+    mid_shard = over_fsdp(grad_mid)
+    q_up, mid_shard, enc_up, ffn_shards = lax.optimization_barrier(
+        (q_up, mid_shard, enc_up, [lax.psum(x, CHIPS) for x in ffn_shards])
+    )
     enc_grad_rows = mul_back(enc_up[:, :d], ck_mat) + mul_back(enc_up[:, d:], cv_mat)
     encoder_grads = gather(enc_grad_rows.astype(BF), CTX)[:frames].astype(F32)
     grad_ckv = grad_of(enc_rows, enc_up)
-    part, grad_gain_two, grad_shift_two = norm_back_two(mul_back(cq_up, cq_mat))
-    up = up + part
-    so_up = up.astype(BF)
-
-    self_dout = mul_back(so_up, so_mat).astype(BF)
-    dout_own = exchange(to_heads(self_dout))
-    grad_mid = jnp.concatenate(
-        [grad_of(mixed, so_up), grad_of(normed_two, cq_up), grad_of(cross_rows, co_up)], axis=1
-    )
-    q_up, k_part, v_part = flash_bwd(
-        q, dout_own, mixed32, lse, k, v, info, hg, piece, kt, True, ctx, q_index, rows_of, "self_bwd"
-    )
-    mid_shard = lax.psum(scatter(grad_mid, "fsdp"), CTX)
-    ckv_shard = lax.psum(scatter(grad_ckv, "fsdp"), CTX)
+    ckv_shard = whole(lax.psum(over_fsdp(on_chip(grad_ckv)), CHIPS))
+    mid_shard = whole(lax.psum(mid_shard, CHIPS))
+    expand_shard, reduce_shard = [whole(x) for x in ffn_shards]
 
     def pick(x, member):
         x = x.reshape(ctx, members, piece, x.shape[-1])
@@ -583,12 +612,12 @@
     kv_up = pick(kv_part, mi).astype(F32)
     for hop in range(1, members):
         kv_up = kv_up + lax.ppermute(
-            pick(kv_part, mi + hop), "m", [(i, (i + hop) % members) for i in range(members)]
+            pick(kv_part, mi + hop), ("p", "c"), [(i, (i + hop) % members) for i in range(members)]
         ).astype(F32)
     qkv_up = jnp.concatenate([q_up, kv_up.astype(BF)], axis=1)
     qkv_rows = to_rows(exchange(qkv_up), 3 * width)
     grad_qkv = grad_of(pick(normed_all, mi), qkv_up)
-    qkv_shard = gather(lax.psum(scatter(grad_qkv, "fsdp"), "m"), "g").reshape(groups, shard, 3, width)
+    qkv_shard = gather(lax.psum(scatter(grad_qkv, "fsdp"), ("p", "c")), "g").reshape(groups, shard, 3, width)
     query_shard, key_shard, value_shard = [
         qkv_shard[:, :, i].transpose(1, 0, 2).reshape(shard, d) for i in range(3)
     ]
@@ -627,7 +656,9 @@
 def solution(mesh):
     ctx, fs = mesh.shape["ctx"], mesh.shape["fsdp"]
     groups = math.gcd(HEADS, ctx // 2)
-    split = Mesh(mesh.devices.reshape(groups, ctx // groups, fs), ("g", "m", "fsdp"))
+    split = Mesh(
+        mesh.devices.reshape(groups, ctx // groups // 2, 2, fs), ("g", "p", "c", "fsdp")
+    )
     rows, slot, vec, mat = P("fsdp", CTX, None), P("fsdp", None, None), P("fsdp"), P("fsdp", None)
     weights = (
         vec, vec, mat, vec, mat, mat, vec, mat, vec, vec, vec, mat, vec, mat, mat, vec, mat, vec,

time: 1020 us -> 891 us (0.87)
  waiting for transfers between devices: 523 us -> 319 us
  other arithmetic: 49.9 us -> 79.5 us
  Pallas kernels: 158 us -> 186 us
  blocking collectives: 98.1 us -> 72.5 us
  local copies, waits for them, and re-layouts: 103 us -> 127 us
  starting transfers between devices: 13.6 us -> 36.4 us
    reduce_scatter x5 -> x2, waiting for transfers between devices: 237 us -> 0.01 us  [scatter(): return lax.psum_scatter(x, axes, scatter_dimension=0, tiled=True)]
    all_gather x1, blocking collectives: 56.6 us -> 31.2 us  [gather(): return lax.all_gather(x, axes, axis=0, tiled=True)]
    all_to_all x0 -> x4, starting transfers between devices: none -> 21.2 us  [over_fsdp(): lax.all_to_all(x.reshape(fs, x.shape[0] // fs, x.shape[1]), 'fsdp', 0, 0)]
    psum x2 -> x3, waiting for transfers between devices: 57.3 us -> 77.6 us  [the longest x1 59.8 us: body(): mid_shard = whole(lax.psum(mid_shard, CHIPS))]
    pallas_call x2, Pallas kernels: 79.1 us -> 97.4 us  [flash_bwd(): pl.pallas_call(functools.partial(bwd_kernel, hg, qt, kt, causal, rows_of)...]
    convert_element_type x0 -> x8, other arithmetic: none -> 17.7 us  [the longest x4 14.3 us: on_chip(): return (half(x, core).astype(F32) + other.astype(F32)).astype(BF)]
    all_to_all x3, waiting for transfers between devices: 20.8 us -> 37 us  [exchange(): return lax.all_to_all(x, CTX, 0, 0, tiled=True)]
    unnamed x131 -> x100, local copies, waits for them, and re-layouts: 45.3 us -> 34.4 us
  transfers between devices with their start and end apart: 19 -> 28, of which waited for: 13 -> 10; matrix products, arithmetic and copies ran while one was open for 13% -> 22% of each run, Pallas kernels for 6% -> 21%
where the time goes in v2:
time: 891 us; the launch traced here: 883 us
  waiting for transfers between devices  319 us (36%)
  Pallas kernels  186 us (21%)
  local copies, waits for them, and re-layouts  127 us (14%)
  other arithmetic  79.5 us (9%)
  blocking collectives  72.5 us (8%)
  matrix products  45.6 us (5%)
  starting transfers between devices  36.4 us (4%)
  between operations  16.2 us (2%)
    all_gather x7, waiting for transfers between devices, gather(): return lax.all_gather(x, axes, axis=0, tiled=True)  197 us
    pallas_call x2, Pallas kernels, flash_bwd(): pl.pallas_call(functools.partial(bwd_kernel, hg, qt, kt, causal, rows_of)...  97.4 us
    psum x1, waiting for transfers between devices, body(): mid_shard = whole(lax.psum(mid_shard, CHIPS))  59.8 us
    pallas_call x2, Pallas kernels, flash_fwd(): pl.pallas_call(functools.partial(fwd_kernel, hg, qt, kt, causal, rows_of)...  54.7 us
    psum x1, blocking collectives, body(): sums = lax.psum(sums, ALL)  41.3 us
    all_to_all x3, waiting for transfers between devices, exchange(): return lax.all_to_all(x, CTX, 0, 0, tiled=True)  37 us
    unnamed x100, local copies, waits for them, and re-layouts  34.4 us
    all_gather x1, blocking collectives, gather(): return lax.all_gather(x, axes, axis=0, tiled=True)  31.2 us
  transfers between devices with their start and end apart: 28, of which 10 were waited for; matrix products, arithmetic and copies ran while one was open for 22% of the time, Pallas kernels for 21%

profile of v2, /device:TPU:0, one launch (start us, length us, event | category | flops | bytes accessed | tf_op | source)
XLA Modules:
  0.0 882.5 jit_solution(10435564687602315853)
XLA Ops:
  29.1 23.5 %all-gather.9.cloned.1.call-done = bf16[768,704]{1,0:T(8,128)(2,1)} async-done(((bf16[192,704]{1,0:T(8,128)(2,1)}), bf16[768,704]{1,0:T(8,128)(2,1)}) %all-gather.9.cloned.1.call-update) | async-done | bytes 1081360 | tf_op jit(solution)/shard_map/all_gather | solution.py:411
  57.0 62.0 %all-gather.21.cloned.1.call-done = bf16[1,4096,768]{2,1,0:T(8,128)(2,1)} async-done(((bf16[1,512,768]{2,1,0:T(8,128)(2,1)}), bf16[1,4096,768]{2,1,0:T(8,128)(2,1)}) %all-gather.21.cloned.1.call-update) | async-done | bytes 6291472 | tf_op jit(solution)/shard_map/all_gather | solution.py:411
  119.0 13.7 %ln_qkv.1 = (bf16[4096,768]{1,0:T(8,128)(2,1)}, bf16[4096,192]{1,0:T(8,128)(2,1)}, bf16[4096,192]{1,0:T(8,128)(2,1)}, bf16[4096,192]{1,0:T(8,128)(2,1)}) custom-call(bf16[4096,768]{1,0:T(8,128)(2,1)} %bitcast.192, bf16[768,576]{1,0:T(8,128)(2,1)} %slice.211.w_ref, f32[1,576]{1,0:T(1,128)} %broadcast_in_dim.76.add_ref, f32[1,768]{1,0:T(1,128)} %get-tuple-element.366.gain_ref, ...), custom_call_target="tpu_custom_call" | custom-call | flops 3623878656 | bytes 17301504 | tf_op jit(solution)/shard_map/ln_qkv/pallas_call | solution.py:310
  132.6 33.9 %self_fwd.1 = (f32[2048,192]{1,0:T(8,128)}, bf16[2048,192]{1,0:T(8,128)(2,1)}, f32[1,8,3,256]{3,2,1,0:T(4,128)}) custom-call(s32[2]{0:T(128)} %pad_add_fusion.info, bf16[4096,192]{1,0:T(8,128)(2,1)} %get-tuple-element.60.q_ref, bf16[4096,192]{1,0:T(8,128)(2,1)} %get-tuple-element.61.k_ref, bf16[4096,192]{1,0:T(8,128)(2,1)} %get-tuple-element.62.v_ref), custom_call_target="tpu_custom_call" | custom-call | flops 12884901888 | bytes 6291456 | tf_op jit(solution)/shard_map/self_fwd/pallas_call | solution.py:210
  175.7 11.2 %all-gather.11.cloned.1.call-done = bf16[768,3840]{1,0:T(8,128)(2,1)} async-done(((bf16[192,3840]{1,0:T(8,128)(2,1)}), bf16[768,3840]{1,0:T(8,128)(2,1)}) %all-gather.11.cloned.1.call-update) | async-done | bytes 5898256 | tf_op jit(solution)/shard_map/all_gather | solution.py:411
  186.9 5.5 convolution_convert_fusion.1.k_ref
  192.4 4.7 add_convert_fusion.2.v_ref
  204.6 20.7 %cross_fwd.1 = (f32[512,768]{1,0:T(8,128)}, bf16[512,768]{1,0:T(8,128)(2,1)}, f32[3,2,4,256]{3,2,1,0:T(4,128)}) custom-call(s32[2]{0:T(128)} %constant.105.clone.info, bf16[512,768]{1,0:T(8,128)(2,1)} %add_convert_fusion.7.q_ref, bf16[1536,768]{1,0:T(8,128)(2,1)} %convolution_convert_fusion.1.k_ref, bf16[1536,768]{1,0:T(8,128)(2,1)} %add_convert_fusion.2.v_ref), custom_call_target="tpu_custom_call" | custom-call | flops 9663676416 | bytes 7864320 | tf_op jit(solution)/shard_map/cross_fwd/pallas_call | solution.py:210
  229.2 16.3 %all-gather.13.cloned.1.call-done.we_ref = bf16[768,3072]{1,0:T(8,128)(2,1)} async-done(((bf16[192,3072]{1,0:T(8,128)(2,1)}), bf16[768,3072]{1,0:T(8,128)(2,1)}) %all-gather.13.cloned.1.call-update) | async-done | bytes 4718608 | tf_op jit(solution)/shard_map/all_gather | solution.py:411
  245.5 58.7 %all-gather.15.cloned.1.call-done.wr_ref = bf16[3072,768]{1,0:T(8,128)(2,1)} async-done(((bf16[768,768]{1,0:T(8,128)(2,1)}), bf16[3072,768]{1,0:T(8,128)(2,1)}) %all-gather.15.cloned.1.call-update) | async-done | bytes 4718608 | tf_op jit(solution)/shard_map/all_gather | solution.py:411
  304.2 20.6 %ffn.1 = (f32[512,768]{1,0:T(8,128)}, f32[512,768]{1,0:T(8,128)}, bf16[768,3072]{1,0:T(8,128)(2,1)}, bf16[3072,768]{1,0:T(8,128)(2,1)}, f32[1,3072]{1,0:T(1,128)}) custom-call(bf16[512,768]{1,0:T(8,128)(2,1)} %add_convert_fusion.6.n_ref, bf16[512,768]{1,0:T(8,128)(2,1)} %get-tuple-element.335.up_ref, bf16[768,3072]{1,0:T(8,128)(2,1)} %all-gather.13.cloned.1.call-done.we_ref, ...), custom_call_target="tpu_custom_call" | custom-call | flops 14495514624 | bytes 23592960 | tf_op jit(solution)/shard_map/ffn/pallas_call | solution.py:354
  348.7 25.2 %all-gather.17.cloned.1.call-done = bf16[768,2304]{1,0:T(8,128)(2,1)} async-done(((bf16[192,2304]{1,0:T(8,128)(2,1)}), bf16[768,2304]{1,0:T(8,128)(2,1)}) %all-gather.17.cloned.1.call-update) | async-done | bytes 3538960 | tf_op jit(solution)/shard_map/all_gather | solution.py:411
  383.0 37.8 %cross_bwd.1 = (bf16[512,768]{1,0:T(8,128)(2,1)}, bf16[1536,768]{1,0:T(8,128)(2,1)}, bf16[1536,768]{1,0:T(8,128)(2,1)}) custom-call(s32[2]{0:T(128)} %constant.105.clone.info, bf16[512,768]{1,0:T(8,128)(2,1)} %add_convert_fusion.7.q_ref, bf16[512,768]{1,0:T(8,128)(2,1)} %convolution_convert_fusion.7.do_ref, f32[512,768]{1,0:T(8,128)} %get-tuple-element.68.o_ref, ...), custom_call_target="tpu_custom_call" | custom-call | flops 24159191040 | bytes 13369344 | tf_op jit(solution)/shard_map/cross_bwd/pallas_call | solution.py:250
  458.3 4.7 all-to-all-start.3
  464.4 37.0 %all-to-all-done.3 = bf16[8,256,192]{1,2,0:T(8,128)(2,1)} async-done(((bf16[8,256,192]{1,2,0:T(8,128)(2,1)}), bf16[8,256,192]{1,2,0:T(8,128)(2,1)}, u32[]{:S(2)}, u32[]{:S(2)}) %all-to-all-start.3) | async-done | bytes 786464 | tf_op jit(solution)/shard_map/all_to_all | solution.py:503
  515.1 59.7 %self_bwd.1 = (bf16[2048,192]{1,0:T(8,128)(2,1)}, bf16[4096,192]{1,0:T(8,128)(2,1)}, bf16[4096,192]{1,0:T(8,128)(2,1)}) custom-call(s32[2]{0:T(128)} %pad_add_fusion.info, bf16[4096,192]{1,0:T(8,128)(2,1)} %get-tuple-element.60.q_ref, bf16[2048,192]{1,0:T(8,128)(2,1)} %bitcast.173, f32[2048,192]{1,0:T(8,128)} %get-tuple-element.75.o_ref, ...), custom_call_target="tpu_custom_call" | custom-call | flops 32212254720 | bytes 10223616 | tf_op jit(solution)/shard_map/self_bwd/pallas_call | solution.py:250
  601.9 5.8 convolution_convert_fusion.5
  610.6 7.8 all-to-all-start.6
  631.4 5.5 all-to-all-done.6
  658.5 59.8 %all-reduce.10.cloned.1.call-done = (bf16[192,1152]{1,0:T(8,128)(2,1)}, bf16[192,768]{1,0:T(8,128)(2,1)}) async-done(((bf16[192,1152]{1,0:T(8,128)(2,1)}, bf16[192,768]{1,0:T(8,128)(2,1)}), (bf16[192,1152]{1,0:T(8,128)(2,1)}, bf16[192,768]{1,0:T(8,128)(2,1)})) %all-reduce.10.cloned.1.call-update) | async-done | bytes 737296 | tf_op jit(solution)/shard_map/psum | solution.py:600
  718.3 17.9 %all-reduce.8.cloned.1.call-done = bf16[192,576]{1,0:T(8,128)(2,1)} async-done(((bf16[192,576]{1,0:T(8,128)(2,1)}), bf16[192,576]{1,0:T(8,128)(2,1)}) %all-reduce.8.cloned.1.call-update) | async-done | bytes 221200 | tf_op jit(solution)/shard_map/psum | solution.py:620
  736.1 31.2 %all_gather.31 = bf16[768,576]{1,0:T(8,128)(2,1)} all-gather(bf16[192,576]{1,0:T(8,128)(2,1)} %all-reduce.8.cloned.1.call-done), channel_id=1, replica_groups=mesh['g'=4,'p'=1,'c'=2,'fsdp'=4] {'g'}, dimensions={0}, use_global_device_ids=true | all-gather | bytes 1105920 | tf_op jit(solution)/shard_map/all_gather | solution.py:411
  803.1 41.3 %psum.44 = f32[17,768]{1,0:T(8,128)S(1)} all-reduce(f32[17,768]{1,0:T(8,128)S(1)} %concatenate.59), channel_id=1, replica_groups=mesh['g'=4,'p'=1,'c'=2,'fsdp'=4] {'g','p','c','fsdp'}, use_global_device_ids=true, to_apply=%region_31.32 | all-reduce | flops 13056 | bytes 104448 | tf_op jit(solution)/shard_map/psum | solution.py:641
  846.5 25.8 %copy.236 = f32[1,1500,768]{2,0,1:T(1,128)} copy(f32[1,1500,768]{2,1,0:T(8,128)S(1)} %fusion.2) | data formatting | bytes 9216000
  (318 shorter events, 236.0 us)
Async XLA Ops:
  7.2 45.4 %all-gather.9.cloned.1.call-start = ((), (), s32[]{:S(2)}) async-start(), calls=%async_computation.9 | async-start | bytes 1474560 | tf_op jit(solution)/shard_map/all_gather | solution.py:411
  22.2 96.8 %all-gather.21.cloned.1.call-start = ((), (), s32[]{:S(2)}) async-start(), calls=%async_computation.18 | async-start | bytes 7077888 | tf_op jit(solution)/shard_map/all_gather | solution.py:411
  22.9 163.9 %all-gather.11.cloned.1.call-start = ((), (), s32[]{:S(2)}) async-start(), calls=%async_computation.10 | async-start | bytes 7372800 | tf_op jit(solution)/shard_map/all_gather | solution.py:411
  24.4 221.1 %all-gather.13.cloned.1.call-start = ((), (), s32[]{:S(2)}) async-start(), calls=%async_computation.11 | async-start | bytes 5898240 | tf_op jit(solution)/shard_map/all_gather | solution.py:411
  25.0 279.2 %all-gather.15.cloned.1.call-start = ((), (), s32[]{:S(2)}) async-start(), calls=%async_computation.12 | async-start | bytes 5898240 | tf_op jit(solution)/shard_map/all_gather | solution.py:411
  25.6 348.4 %all-gather.17.cloned.1.call-start = ((), (), s32[]{:S(2)}) async-start(), calls=%async_computation.13 | async-start | bytes 4423680 | tf_op jit(solution)/shard_map/all_gather | solution.py:411
  168.8 28.3 %all-to-all-start = ((bf16[8,256,192]{1,2,0:T(8,128)(2,1)}), bf16[8,256,192]{1,2,0:T(8,128)(2,1)S(1)}, u32[]{:S(2)}, u32[]{:S(2)}) async-start(bf16[8,256,192]{1,2,0:T(8,128)(2,1)} %copy.217), calls=%async_computation | async-start | bytes 1572864 | tf_op jit(solution)/shard_map/all_to_all | solution.py:503
  331.5 42.4 %collective-permute-start = (bf16[768,1536]{1,0:T(8,128)(2,1)}, bf16[768,1536]{1,0:T(8,128)(2,1)}, u32[]{:S(2)}, u32[]{:S(2)}) collective-permute-start(bf16[768,1536]{1,0:T(8,128)(2,1)} %constant_dynamic-slice_fusion.4), channel_id=1, source_target_pairs={{0,4},{4,0},{1,5},{5,1},{2,6},{6,2},{3,7},{7,3},{8,12},{12,8},{9,1... | collective-permute-start | bytes 7077896 | tf_op jit(solution)/shard_map/ppermute | solution.py:521
  337.0 41.4 %all-to-all-start.2 = ((bf16[4,768,384]{2,1,0:T(8,128)(2,1)}), bf16[4,768,384]{2,1,0:T(8,128)(2,1)}, u32[]{:S(2)}, u32[]{:S(2)}) async-start(bf16[4,768,384]{2,1,0:T(8,128)(2,1)} %bitcast.150), calls=%async_computation.2 | async-start | bytes 4718592 | tf_op jit(solution)/shard_map/all_to_all | solution.py:525
  378.4 45.3 %all-to-all-start.1 = ((bf16[4,192,1536]{2,1,0:T(8,128)(2,1)}), bf16[4,192,1536]{2,1,0:T(8,128)(2,1)}, u32[]{:S(2)}, u32[]{:S(2)}) async-start(bf16[4,192,1536]{2,1,0:T(8,128)(2,1)} %bitcast.151), calls=%async_computation.1 | async-start | bytes 4718592 | tf_op jit(solution)/shard_map/all_to_all | solution.py:525
  383.0 208.8 %all-reduce.12.cloned.1.call-start = ((), (), s32[]{:S(2)}) async-start(), calls=%async_computation.20 | async-start | bytes 2359296 | tf_op jit(solution)/shard_map/psum | solution.py:594
  426.8 164.9 %reduce-scatter.3.cloned.1.call-start = ((), (), s32[]{:S(2)}) async-start(), calls=%async_computation.14 | async-start | bytes 5308416 | tf_op jit(solution)/shard_map/reduce_scatter | solution.py:415
  444.9 58.8 %collective-permute-start.2 = (bf16[768,1152]{0,1:T(8,128)(2,1)}, bf16[768,1152]{0,1:T(8,128)(2,1)}, u32[]{:S(2)}, u32[]{:S(2)}) collective-permute-start(bf16[768,1152]{0,1:T(8,128)(2,1)} %constant_dynamic-slice_fusion.2), channel_id=1, source_target_pairs={{0,4},{4,0},{1,5},{5,1},{2,6},{6,2},{3,7},{7,3},{8,12},{12,8},{9,1... | collective-permute-start | bytes 5308424 | tf_op jit(solution)/shard_map/ppermute | solution.py:521
  458.3 43.1 %all-to-all-start.3 = ((bf16[8,256,192]{1,2,0:T(8,128)(2,1)}), bf16[8,256,192]{1,2,0:T(8,128)(2,1)}, u32[]{:S(2)}, u32[]{:S(2)}) async-start(bf16[8,256,192]{1,2,0:T(8,128)(2,1)} %bitcast.163), calls=%async_computation.3 | async-start | bytes 1572864 | tf_op jit(solution)/shard_map/all_to_all | solution.py:503
  510.7 78.4 %all-to-all-start.4 = ((bf16[4,192,1152]{2,1,0:T(8,128)(2,1)}), bf16[4,192,1152]{2,1,0:T(8,128)(2,1)}, u32[]{:S(2)}, u32[]{:S(2)}) async-start(bf16[4,192,1152]{2,1,0:T(8,128)(2,1)} %bitcast.22), calls=%async_computation.4 | async-start | bytes 3538944 | tf_op jit(solution)/shard_map/all_to_all | solution.py:525
  515.1 134.8 %reduce-scatter.5.cloned.1.call-start = ((), (), s32[]{:S(2)}) async-start(), calls=%async_computation.16 | async-start | bytes 1228800 | tf_op jit(solution)/shard_map/reduce_scatter | solution.py:415
  610.6 26.3 %all-to-all-start.6 = ((bf16[4,192,768]{2,1,0:T(8,128)(2,1)}), bf16[4,192,768]{2,1,0:T(8,128)(2,1)S(1)}, u32[]{:S(2)}, u32[]{:S(2)}) async-start(bf16[4,192,768]{2,1,0:T(8,128)(2,1)} %bitcast.160), calls=%async_computation.8 | async-start | bytes 2359296 | tf_op jit(solution)/shard_map/all_to_all | solution.py:525
  618.4 99.9 %all-reduce.10.cloned.1.call-start = ((), (), s32[]{:S(2)}) async-start(), calls=%async_computation.19 | async-start | bytes 1474560 | tf_op jit(solution)/shard_map/psum | solution.py:600
  630.8 24.9 %collective-permute-start.8 = (bf16[768,384]{1,0:T(8,128)(2,1)}, bf16[768,384]{1,0:T(8,128)(2,1)}, u32[]{:S(2)}, u32[]{:S(2)}) collective-permute-start(bf16[768,384]{1,0:T(8,128)(2,1)} %get-tuple-element.92), channel_id=1, source_target_pairs={{0,4},{4,0},{1,5},{5,1},{2,6},{6,2},{3,7},{7,3},{8,12},{12,8},{9,1... | collective-permute-start | bytes 1769480 | tf_op jit(solution)/shard_map/ppermute | solution.py:529
  630.9 21.8 %collective-permute-start.7 = (bf16[192,1536]{1,0:T(8,128)(2,1)}, bf16[192,1536]{1,0:T(8,128)(2,1)}, u32[]{:S(2)}, u32[]{:S(2)}) collective-permute-start(bf16[192,1536]{1,0:T(8,128)(2,1)} %get-tuple-element.91), channel_id=1, source_target_pairs={{0,4},{4,0},{1,5},{5,1},{2,6},{6,2},{3,7},{7,3},{8,12},{12,8},{9,1... | collective-permute-start | bytes 1769480 | tf_op jit(solution)/shard_map/ppermute | solution.py:529
  640.8 153.4 %all-to-all-start.5 = ((bf16[8,256,576]{1,2,0:T(8,128)(2,1)}), bf16[8,256,576]{1,2,0:T(8,128)(2,1)S(1)}, u32[]{:S(2)}, u32[]{:S(2)}) async-start(bf16[8,256,576]{1,2,0:T(8,128)(2,1)} %bitcast.153), calls=%async_computation.6 | async-start | bytes 4718592 | tf_op jit(solution)/shard_map/all_to_all | solution.py:503
  645.3 90.9 %all-reduce.8.cloned.1.call-start = ((), (), s32[]{:S(2)}) async-start(), calls=%async_computation.17 | async-start | bytes 491520 | tf_op jit(solution)/shard_map/psum | solution.py:620
  649.9 194.6 %all-gather.19.cloned.1.call-start = ((), (), s32[]{:S(2)}) async-start(), calls=%async_computation.15 | async-start | bytes 2654208 | tf_op jit(solution)/shard_map/all_gather | solution.py:411
  718.3 72.3 %collective-permute-start.6 = (bf16[192,768]{1,0:T(8,128)(2,1)}, bf16[192,768]{1,0:T(8,128)(2,1)}, u32[]{:S(2)}, u32[]{:S(2)}) collective-permute-start(bf16[192,768]{1,0:T(8,128)(2,1)} %get-tuple-element.331), channel_id=1, source_target_pairs={{0,4},{4,0},{1,5},{5,1},{2,6},{6,2},{3,7},{7,3},{8,12},{12,8},{9,1... | collective-permute-start | bytes 884744 | tf_op jit(solution)/shard_map/ppermute | solution.py:529
  (51 other events, 204.8 us)
Sparse Core Ops, SparseCore 0:
  22.3 30.2 all-gather.8
  54.2 64.6 all-gather.20
  121.4 65.4 all-gather.10
  188.6 56.9 all-gather.12
  247.2 56.9 all-gather.14
  305.9 68.0 all-gather.16
  426.9 74.6 all-reduce.11
  504.0 53.7 reduce-scatter.2
  607.8 39.2 reduce-scatter.4
  650.5 67.7 all-reduce.9
  720.6 15.4 all-reduce.7
  737.6 40.2 all-gather.18
